TPU v7x, 256 devices: a whole 4x4x8 slice. The times are simulated.
256 devices in a mesh: seq: 32 (over x, y, core), exp: 8 (over z).
Axes of the slice: x: 4, y: 4, z: 8, core: 2. Of those that a mesh axis runs over, the one named last changes fastest.
Arguments:
- tokens: bfloat16 [96, 4, 1024], P('exp'), may hold values from -48 to 48
- attn_gain: float32 [1024], replicated, may hold values from 0.1 to 1.9
- w_qkv: bfloat16 [3072, 1024], P('seq'), may hold values from -0.1875 to 0.1875
- window_cache: bfloat16 [2, 96, 4096, 1024], P(None, 'exp', 'seq'), may hold values from -180 to 180
- sink_cache: bfloat16 [2, 96, 4, 1024], P(None, 'exp'), may hold values from -6 to 6
- lengths: int32 [96], P('exp'), may hold values from 8 to 16384, as said below
- w_out: bfloat16 [1024, 1024], P('seq'), may hold values from -0.1875 to 0.1875
- moe_gain: float32 [1024], replicated, may hold values from 0.1 to 1.9
- router: bfloat16 [1024, 16], replicated, may hold values from -0.1875 to 0.1875
- expert_ids: int32 [96, 4, 2], P('exp'), may hold values from 0 to 15, all different within a row
- slot_order: int32 [8, 48], P('exp'), may hold values from 0 to 47, each once within a row
- expert_in: bfloat16 [2, 8, 5632, 1024], P(None, 'exp', 'seq'), may hold values from -0.1875 to 0.1875
- expert_down: bfloat16 [8, 5632, 1024], P('exp', 'seq'), may hold values from -0.109375 to 0.109375
Outputs:
- output: bfloat16 [96, 4, 1024], P('exp')
Inputs may be any that keep to these rules, and one draw needn't show every extreme that they name: `lengths`: at least one request holds 16384 tokens. `expert_ids`: the 2 experts of a token differ, and every expert is named by some token. `slot_order`: each group's row holds every number of 0 to 47 once.
All inputs are finite; a program needn't handle non-finite values.
Results may differ from a plain program's by a relative error of at most 0.0083.
The roundings to bfloat16 on the way count: a program that leaves them out, or rounds other values in their place, can miss the bound.
Values may be sent and summed in bfloat16 or wider, within the bound.
A program may use at most 64 MiB of HBM per device.

v0:
```python
import jax
import jax.numpy as jnp
from jax import lax
from jax.sharding import PartitionSpec as P

HEADS = 16
HD = 64
EXPERTS = 16
TOPK = 2
SINKS = 4
WIN = 4096
CAP = 8


EPSILON = 1e-06
MASKED = -1e30


def rms_scale(values, gain_row):
    widened = values.astype(jnp.float32)
    inverse = lax.rsqrt(jnp.mean(widened * widened, axis=-1, keepdims=True) + EPSILON)
    return (widened * inverse * gain_row).astype(jnp.bfloat16)


def by_heads(values, factor):
    shaped = values.reshape(factor.shape + (values.shape[-1] // factor.shape[-1],))
    return (shaped * factor[..., None]).reshape(values.shape)


def expert_tail(gate_up, down_rows, own_expert, local_experts):
    hidden = (jax.nn.gelu(gate_up[0], approximate=True) * gate_up[1]).astype(jnp.bfloat16)
    outputs = jnp.einsum("nkf,fd->nkd", hidden, down_rows, preferred_element_type=jnp.float32)
    placing = (jnp.arange(local_experts, dtype=jnp.int32) == own_expert).astype(jnp.float32)
    return outputs[:, None, :, :] * placing[None, :, None, None]


def body(
    tokens,
    attn_gain,
    w_qkv,
    window_cache,
    sink_cache,
    lengths,
    w_out,
    moe_gain,
    router,
    expert_ids,
    slot_order,
    expert_in,
    expert_down,
):
    requests, step_count, model_width = tokens.shape
    row_count = requests * step_count
    seq_index = lax.axis_index("seq")
    seq_count = lax.axis_size("seq")
    group_count = lax.axis_size("exp")
    local_experts = EXPERTS // group_count
    own_expert = seq_index // (seq_count // local_experts)
    in_rows = expert_in[:, 0]
    down_rows = expert_down[0]
    contract = (((1,), (1,)), ((), ()))
    flat_rows = tokens.reshape(row_count, model_width)
    normed_attn = rms_scale(flat_rows, attn_gain)
    local_mix = lax.dot_general(
        normed_attn, w_qkv, contract, preferred_element_type=jnp.float32
    ).astype(jnp.bfloat16)
    mixed_rows = lax.all_gather(local_mix, "seq", axis=1, tiled=True).reshape(
        requests, step_count, 3, HEADS, HD
    )
    queries = mixed_rows[:, :, 0]
    new_keys = mixed_rows[:, :, 1]
    new_values = mixed_rows[:, :, 2]
    score_scale = HD ** (-0.5)
    slot_span = window_cache.shape[2]
    slot_ids = seq_index * slot_span + jnp.arange(slot_span, dtype=jnp.int32)
    cache_keys = window_cache[0].reshape(requests, slot_span, HEADS, HD)
    cache_values = window_cache[1].reshape(requests, slot_span, HEADS, HD)
    window_scores = (
        jnp.einsum("rshe,rwhe->rshw", queries, cache_keys, preferred_element_type=jnp.float32)
        * score_scale
    )
    filled = jnp.minimum(WIN, lengths - SINKS)
    step_ids = jnp.arange(step_count, dtype=jnp.int32)
    written = (lengths[:, None] + step_ids[None, :] - SINKS) % WIN
    overwritten = (
        jnp.cumsum((slot_ids[None, None, :] == written[:, :, None]).astype(jnp.int32), axis=1) > 0
    )
    window_live = (
        (slot_ids[None, None, :] < filled[:, None, None]) & jnp.logical_not(overwritten)
    )[:, :, None, :]
    sink_keys = sink_cache[0].reshape(requests, SINKS, HEADS, HD)
    sink_values = sink_cache[1].reshape(requests, SINKS, HEADS, HD)
    local_keys = jnp.concatenate([sink_keys, new_keys], axis=1)
    local_values = jnp.concatenate([sink_values, new_values], axis=1)
    local_scores = (
        jnp.einsum("rshe,rkhe->rshk", queries, local_keys, preferred_element_type=jnp.float32)
        * score_scale
    )
    causal = jnp.concatenate(
        [jnp.ones((step_count, SINKS), jnp.bool_), step_ids[None, :] <= step_ids[:, None]], axis=1
    )
    local_live = causal[None, :, None, :] & (seq_index == 0)
    peak_score = jnp.maximum(
        jnp.max(jnp.where(window_live, window_scores, MASKED), axis=-1),
        jnp.max(jnp.where(local_live, local_scores, MASKED), axis=-1),
    )
    window_exp = jnp.where(window_live, jnp.exp(window_scores - peak_score[..., None]), 0.0)
    local_exp = jnp.where(local_live, jnp.exp(local_scores - peak_score[..., None]), 0.0)
    weight_sum = jnp.sum(window_exp, axis=-1) + jnp.sum(local_exp, axis=-1)
    weighted = jnp.einsum(
        "rshw,rwhe->rshe",
        window_exp.astype(jnp.bfloat16),
        cache_values,
        preferred_element_type=jnp.float32,
    )
    weighted = weighted + jnp.einsum(
        "rshk,rkhe->rshe",
        local_exp.astype(jnp.bfloat16),
        local_values,
        preferred_element_type=jnp.float32,
    )
    weighted = weighted.reshape(requests, step_count, model_width)
    overall = lax.pmax(peak_score, "seq")
    factor = jnp.exp(peak_score - overall)
    weight_sum, weighted = (
        lax.psum((weight_sum * factor).astype(jnp.bfloat16), "seq").astype(jnp.float32),
        lax.psum(by_heads(weighted, factor).astype(jnp.bfloat16), "seq").astype(jnp.float32),
    )
    attended = by_heads(weighted, 1.0 / weight_sum).astype(jnp.bfloat16)
    local_proj = lax.dot_general(
        attended.reshape(row_count, model_width),
        w_out,
        contract,
        preferred_element_type=jnp.float32,
    ).astype(jnp.bfloat16)
    projected = lax.all_gather(local_proj, "seq", axis=1, tiled=True)
    residual = flat_rows.astype(jnp.float32) + projected.astype(jnp.float32)
    normed_moe = rms_scale(residual, moe_gain)
    logits = jnp.dot(normed_moe, router, preferred_element_type=jnp.float32)
    chosen = expert_ids.reshape(row_count, TOPK)
    onehot = (chosen[:, :, None] == jnp.arange(EXPERTS, dtype=jnp.int32)).astype(jnp.float32)
    gate_values = jax.nn.sigmoid(jnp.sum(onehot * logits[:, None, :], axis=-1))
    priority = slot_order[0]
    earlier = (priority[None, :] < priority[:, None]).astype(jnp.float32)
    counts = jnp.dot(earlier, jnp.sum(onehot, axis=1), precision=lax.Precision.HIGHEST)
    position = jnp.sum(onehot * counts[:, None, :], axis=-1).astype(jnp.int32)
    column = chosen * CAP + position
    select = (
        (column[:, :, None] == jnp.arange(EXPERTS * CAP, dtype=jnp.int32))
        & (position < CAP)[:, :, None]
    ).astype(jnp.bfloat16)
    dispatch = jnp.sum(select, axis=1)
    buffer = lax.dot_general(
        dispatch, normed_moe, (((0,), (0,)), ((), ())), preferred_element_type=jnp.float32
    ).astype(jnp.bfloat16)
    buffer = buffer.reshape(group_count, local_experts, CAP, model_width)
    own_rows = lax.dynamic_index_in_dim(
        lax.all_to_all(buffer, "exp", split_axis=0, concat_axis=0, tiled=True),
        own_expert,
        1,
        keepdims=False,
    )
    gate_up = jnp.einsum("nkd,pfd->pnkf", own_rows, in_rows, preferred_element_type=jnp.float32)
    expert_part = expert_tail(gate_up, down_rows, own_expert, local_experts)
    summed = lax.psum(expert_part.astype(jnp.bfloat16), "seq")
    returned = lax.all_to_all(summed, "exp", split_axis=0, concat_axis=0, tiled=True).reshape(
        EXPERTS * CAP, model_width
    )
    picked = jnp.einsum("rkc,cd->rkd", select, returned, preferred_element_type=jnp.float32)
    final_rows = (residual + jnp.sum(gate_values[:, :, None] * picked, axis=1)).astype(jnp.bfloat16)
    result = final_rows.reshape(requests, step_count, model_width)
    return result


def solution(mesh):
    in_specs = (
        P("exp", None, None),
        P(),
        P("seq", None),
        P(None, "exp", "seq", None),
        P(None, "exp", None, None),
        P("exp"),
        P("seq", None),
        P(),
        P(),
        P("exp", None, None),
        P("exp", None),
        P(None, "exp", "seq", None),
        P("exp", "seq", None),
    )
    out_specs = P("exp", None, None)
    return jax.shard_map(body, mesh=mesh, in_specs=in_specs, out_specs=out_specs, check_vma=False)
```

profile of v0, /device:TPU:1, one launch (start us, length us, event | category | flops | bytes accessed | tf_op | source)
XLA Modules:
  0.0 495.7 jit_solution(1817082701008093470)
XLA Ops:
  6.5 0.8 add_select_fusion
  7.3 0.7 add_minimum_fusion
  8.0 0.9 reshape.165
  8.9 1.0 multiply_reduce_fusion.1
  10.2 6.6 %fusion.66 = (bf16[1,12,128,1024]{3,2,1,0:T(8,128)(2,1)}, bf16[1,12,128,1024]{3,2,1,0:T(8,128)(2,1)}) fusion(bf16[2,12,128,1024]{3,2,1,0:T(8,128)(2,1)} %param.16), kind=kLoop, calls=%fused_computation.111 | loop fusion | bytes 12582912 | tf_op jit(solution)/shard_map/slice | solution.py:77
  16.8 4.8 copy.86
  21.9 26.5 %all-gather = bf16[32,96,48]{1,2,0:T(8,128)(2,1)S(1)} all-gather(bf16[1,96,48]{1,2,0:T(8,128)(2,1)S(1)} %fusion.6), channel_id=1, replica_groups=mesh['seq'=32,'exp'=8] {'seq'}, dimensions={0}, use_global_device_ids=true | all-gather | bytes 304128 | tf_op jit(solution)/shard_map/all_gather | solution.py:67
  49.6 2.9 select_reduce_fusion.1
  54.1 120.9 %pmax.7 = f32[12,4,16]{2,1,0:T(4,128)S(1)} all-reduce(f32[12,4,16]{2,1,0:T(4,128)S(1)} %max.9), channel_id=1, replica_groups=mesh['seq'=32,'exp'=8] {'seq'}, use_global_device_ids=true, to_apply=%region_4.5 | all-reduce | flops 768 | bytes 6144 | tf_op jit(solution)/shard_map/pmax | solution.py:123
  175.6 0.5 fusion.18
  176.6 4.7 copy.92
  182.1 3.7 fusion.4
  185.8 0.8 convert_element_type.106
  186.7 123.9 %psum.22 = bf16[12,4,16]{2,1,0:T(4,128)(2,1)S(1)} all-reduce(bf16[12,4,16]{2,1,0:T(4,128)(2,1)S(1)} %get-tuple-element.7), channel_id=1, replica_groups=mesh['seq'=32,'exp'=8] {'seq'}, use_global_device_ids=true, to_apply=%region_8.9 | all-reduce | flops 768 | bytes 3072 | tf_op jit(solution)/shard_map/psum | solution.py:126
  311.4 0.9 multiply_convert_fusion.2
  312.5 27.6 %all_gather.7 = bf16[48,1024]{0,1:T(8,128)(2,1)S(1)} all-gather(bf16[48,32]{0,1:T(8,128)(2,1)S(1)} %convolution_convert_fusion.2), channel_id=1, replica_groups=mesh['seq'=32,'exp'=8] {'seq'}, dimensions={1}, use_global_device_ids=true | all-gather | bytes 101376 | tf_op jit(solution)/shard_map/all_gather | solution.py:136
  340.8 1.0 convolution_convert_fusion
  341.7 8.2 %all-to-all-start = ((bf16[8,2,8,1024]{3,2,1,0:T(8,128)(2,1)}), bf16[8,2,8,1024]{3,2,1,0:T(8,128)(2,1)S(1)}, u32[]{:S(2)}, u32[]{:S(2)}) async-start(bf16[8,2,8,1024]{3,2,1,0:T(8,128)(2,1)} %bitcast.13), calls=%async_computation | async-start | bytes 524288 | tf_op jit(solution)/shard_map/all_to_all | solution.py:158
  350.0 12.2 %all-to-all-done = bf16[8,2,8,1024]{3,2,1,0:T(8,128)(2,1)S(1)} async-done(((bf16[8,2,8,1024]{3,2,1,0:T(8,128)(2,1)}), bf16[8,2,8,1024]{3,2,1,0:T(8,128)(2,1)S(1)}, u32[]{:S(2)}, u32[]{:S(2)}) %all-to-all-start) | async-done | bytes 262176 | tf_op jit(solution)/shard_map/all_to_all | solution.py:158
  362.7 0.8 multiply_convert_fusion
  363.5 107.1 %all-reduce.6.cloned.1.call-done = bf16[8,2,8,1024]{3,2,1,0:T(8,128)(2,1)} async-done(((bf16[8,2,8,1024]{3,2,1,0:T(8,128)(2,1)}), bf16[8,2,8,1024]{3,2,1,0:T(8,128)(2,1)}) %all-reduce.6.cloned.1.call-update) | async-done | bytes 262160 | tf_op jit(solution)/shard_map/psum | solution.py:165
  470.7 6.7 %all-to-all-start.1 = ((bf16[8,2,8,1024]{3,2,1,0:T(8,128)(2,1)}), bf16[8,2,8,1024]{3,2,1,0:T(8,128)(2,1)S(1)}, u32[]{:S(2)}, u32[]{:S(2)}) async-start(bf16[8,2,8,1024]{3,2,1,0:T(8,128)(2,1)} %all-reduce.6.cloned.1.call-done), calls=%async_computation.1 | async-start | bytes 524288 | tf_op jit(solution)/shard_map/all_to_all | solution.py:166
  477.4 10.4 %all-to-all-done.1 = bf16[8,2,8,1024]{3,2,1,0:T(8,128)(2,1)S(1)} async-done(((bf16[8,2,8,1024]{3,2,1,0:T(8,128)(2,1)}), bf16[8,2,8,1024]{3,2,1,0:T(8,128)(2,1)S(1)}, u32[]{:S(2)}, u32[]{:S(2)}) %all-to-all-start.1) | async-done | bytes 262176 | tf_op jit(solution)/shard_map/all_to_all | solution.py:166
  488.1 0.7 reshape.164
  (82 shorter events, 7.6 us)
Async XLA Ops:
  6.5 355.6 %copy-start = (bf16[2,1,176,1024]{3,2,1,0:T(8,128)(2,1)S(1)}, bf16[2,1,176,1024]{3,2,1,0:T(8,128)(2,1)}, u32[]{:S(2)}) copy-start(bf16[2,1,176,1024]{3,2,1,0:T(8,128)(2,1)} %param.24) | copy-start | bytes 2162692
  6.5 304.8 %all-reduce.4.cloned.1.call-start = ((), (), s32[]{:S(2)}) async-start(), calls=%async_computation.2 | async-start | bytes 196608 | tf_op jit(solution)/shard_map/psum | solution.py:127
  16.8 4.9 copy-start.2
  16.8 4.9 copy-start.6
  49.0 3.7 copy-start.3
  182.0 128.5 %copy-start.8 = (s32[12,4,2]{0,2,1:T(2,128)S(1)}, s32[12,4,2]{0,2,1:T(2,128)}, u32[]{:S(2)}) copy-start(s32[12,4,2]{0,2,1:T(2,128)} %param.22) | copy-start | bytes 1156
  182.0 128.7 %copy-start.9 = (s32[1,48]{1,0:T(1,128)S(1)}, s32[1,48]{1,0:T(1,128)}, u32[]{:S(2)}) copy-start(s32[1,48]{1,0:T(1,128)} %param.23) | copy-start | bytes 580
  182.0 130.3 %copy-start.4 = (bf16[32,1024]{1,0:T(8,128)(2,1)S(1)}, bf16[32,1024]{1,0:T(8,128)(2,1)}, u32[]{:S(2)}) copy-start(bf16[32,1024]{1,0:T(8,128)(2,1)} %param.19) | copy-start | bytes 196612
  182.1 158.3 %copy-start.7 = (f32[1024]{0:T(1024)S(1)}, f32[1024]{0:T(1024)}, u32[]{:S(2)}) copy-start(f32[1024]{0:T(1024)} %param.20) | copy-start | bytes 12292
  185.8 154.7 %copy-start.5 = (bf16[1024,16]{0,1:T(8,128)(2,1)S(1)}, bf16[1024,16]{0,1:T(8,128)(2,1)}, u32[]{:S(2)}) copy-start(bf16[1024,16]{0,1:T(8,128)(2,1)} %param.21) | copy-start | bytes 98308
  185.8 176.7 %copy-start.1 = (bf16[1,176,1024]{2,1,0:T(8,128)(2,1)S(1)}, bf16[1,176,1024]{2,1,0:T(8,128)(2,1)}, u32[]{:S(2)}) copy-start(bf16[1,176,1024]{2,1,0:T(8,128)(2,1)} %param.25) | copy-start | bytes 1081348
  341.7 20.4 %all-to-all-start = ((bf16[8,2,8,1024]{3,2,1,0:T(8,128)(2,1)}), bf16[8,2,8,1024]{3,2,1,0:T(8,128)(2,1)S(1)}, u32[]{:S(2)}, u32[]{:S(2)}) async-start(bf16[8,2,8,1024]{3,2,1,0:T(8,128)(2,1)} %bitcast.13), calls=%async_computation | async-start | bytes 524288 | tf_op jit(solution)/shard_map/all_to_all | solution.py:158
  349.9 120.8 %all-reduce.6.cloned.1.call-start = ((), (), s32[]{:S(2)}) async-start(), calls=%async_computation.3 | async-start | bytes 524288 | tf_op jit(solution)/shard_map/psum | solution.py:165
  470.7 17.2 %all-to-all-start.1 = ((bf16[8,2,8,1024]{3,2,1,0:T(8,128)(2,1)}), bf16[8,2,8,1024]{3,2,1,0:T(8,128)(2,1)S(1)}, u32[]{:S(2)}, u32[]{:S(2)}) async-start(bf16[8,2,8,1024]{3,2,1,0:T(8,128)(2,1)} %all-reduce.6.cloned.1.call-done), calls=%async_computation.1 | async-start | bytes 524288 | tf_op jit(solution)/shard_map/all_to_all | solution.py:166
Sparse Core Ops, SparseCore 0:
  186.8 112.1 all-reduce.3
  363.7 106.9 all-reduce.5
where the time goes:
time: 497 us; the launch traced here: 496 us
  blocking collectives  299 us (60%)
  waiting for transfers between devices  130 us (26%)
  local copies, waits for them, and re-layouts  22.1 us (4%)
  starting transfers between devices  15 us (3%)
  between operations  13.8 us (3%)
  matrix products  10.1 us (2%)
  other arithmetic  6.1 us (1%)
    psum x1, blocking collectives, body(): lax.psum((weight_sum * factor).astype(jnp.bfloat16), 'seq')  124 us
    pmax x1, blocking collectives, body(): overall = lax.pmax(peak_score, 'seq')  121 us
    psum x1, waiting for transfers between devices, body(): summed = lax.psum(expert_part.astype(jnp.bfloat16), 'seq')  107 us
    all_gather x1, blocking collectives, body(): projected = lax.all_gather(local_proj, 'seq', axis=1, tiled=True)  27.6 us
    all_gather x1, blocking collectives, body(): lax.all_gather(local_mix, 'seq', axis=1, tiled=True)  26.5 us
    all_to_all x1, waiting for transfers between devices, body(): lax.all_to_all(buffer, 'exp', split_axis=0, concat_axis=0, tiled=True)  12.2 us
    slice x2, local copies, waits for them, and re-layouts, body(): cache_values = window_cache[1].reshape(requests, slot_span, HEADS, HD)  11.3 us
    all_to_all x1, waiting for transfers between devices, body(): lax.all_to_all(summed, 'exp', split_axis=0, concat_axis=0, tiled=True)  10.4 us
  transfers between devices with their start and end apart: 4, of which 3 were waited for; matrix products, arithmetic and copies ran while one was open for 0% of the time, Pallas kernels for 0%

commit v1 on v0

v1 whole, which is shorter than its diff:
```python
import functools

import jax
import jax.numpy as jnp
from jax import lax
from jax.experimental import pallas as pl
from jax.experimental.pallas import tpu as pltpu
from jax.sharding import PartitionSpec as P

HEADS = 16
HD = 64
EXPERTS = 16
SINKS = 4
WIN = 4096
CAP = 8
STEPS = 4
EPSILON = 1e-06
MASKED = -1e30
MESH = pl.DeviceIdType.MESH
F32 = jnp.float32
BF16 = jnp.bfloat16
LAST = (((1,), (1,)), ((), ()))


def iota(shape, axis):
    return lax.broadcasted_iota(jnp.int32, shape, axis)


def wait_bytes(ref, sem):
    pltpu.make_async_copy(ref, ref, sem).wait()


def layer_kernel(
    seq_count,
    group_count,
    tokens_ref,
    attn_gain_ref,
    w_qkv_ref,
    cache_hbm,
    sink_ref,
    lengths_ref,
    w_out_ref,
    moe_gain_ref,
    router_ref,
    ids_ref,
    order_ref,
    in_hbm,
    down_hbm,
    out_ref,
    kv,
    win,
    down,
    x_tok,
    idcol,
    mix,
    qkv_in,
    qkv,
    q4,
    part_out,
    part_in,
    sinks,
    att_in,
    w_rows,
    proj_in,
    disp_out,
    disp_in,
    exp_out,
    exp_in,
    back_out,
    back_in,
    fin_in,
    kv_sem,
    wt_sem,
    loc_sem,
    send_sem,
    recv_sem,
):
    s = lax.axis_index("seq")
    z = lax.axis_index("exp")
    t = s // 4
    rg = lax.rem(s, 4)
    half = s // 16
    owner16 = lax.rem(s, 16)
    gh = owner16 // 8
    owner8 = 8 * half + lax.rem(s, 8)

    barrier = pltpu.get_barrier_semaphore()

    def greet_plane(k, _):
        pl.semaphore_signal(
            barrier, inc=1, device_id=(lax.rem(s + k, seq_count), z), device_id_type=MESH
        )
        return 0

    def greet_line(k, _):
        pl.semaphore_signal(
            barrier, inc=1, device_id=(s, lax.rem(z + k, group_count)), device_id_type=MESH
        )
        return 0

    lax.fori_loop(1, seq_count, greet_plane, 0)
    lax.fori_loop(1, group_count, greet_line, 0)

    for part in range(3):
        for which in range(2):
            pltpu.make_async_copy(
                cache_hbm.at[which, pl.ds(4 * part, 4)],
                kv.at[which, pl.ds(4 * part, 4)],
                kv_sem.at[which, part],
            ).start()
    pltpu.make_async_copy(in_hbm.at[:, 0], win, wt_sem.at[0]).start()
    pltpu.make_async_copy(down_hbm.at[0], down, wt_sem.at[1]).start()

    def rcopy(src, dst, stage, dest_s, dest_z):
        pltpu.make_async_remote_copy(
            src_ref=src,
            dst_ref=dst,
            send_sem=send_sem.at[stage],
            recv_sem=recv_sem.at[stage],
            device_id=(dest_s, dest_z),
            device_id_type=MESH,
        ).start()

    def to_plane(src, dst, stage):
        def send(k, _):
            rcopy(src, dst, stage, lax.rem(s + k, seq_count), z)
            return 0

        lax.fori_loop(1, seq_count, send, 0)

    for r in range(12):
        x_tok[4 * r : 4 * r + 4, :] = tokens_ref[r].astype(F32)
    x = x_tok[...]
    inverse = lax.rsqrt(jnp.mean(x * x, axis=-1, keepdims=True) + EPSILON)
    normed = (x * inverse * attn_gain_ref[...]).astype(BF16)
    own_mix = lax.dot_general(normed, w_qkv_ref[...], LAST, preferred_element_type=F32)
    mix[...] = jnp.concatenate([own_mix, jnp.zeros((48, 32), F32)], axis=1).astype(BF16)

    pl.semaphore_wait(barrier, seq_count - 1 + group_count - 1)
    to_plane(mix, qkv_in.at[s], 0)
    qkv_in[s] = mix[...]
    w_rows[rg] = w_out_ref[...]
    for k in range(1, 4):
        rcopy(w_out_ref, w_rows.at[rg], 1, 4 * t + lax.rem(rg + k, 4), z)

    for r in range(12):
        idcol[4 * r : 4 * r + 4, :] = ids_ref[r]
    eye = iota((48, 48), 0) == iota((48, 48), 1)
    prio_row = order_ref[...]
    prio_col = jnp.sum(jnp.where(eye, prio_row, 0), axis=1, keepdims=True)
    earlier = (prio_row < prio_col).astype(F32).astype(BF16)
    expert_lane = iota((48, EXPERTS), 1)
    ids = idcol[...]
    onehots = []
    for c in range(2):
        onehots.append((expert_lane == ids[:, c : c + 1]).astype(F32))
    counts = jnp.dot(earlier, (onehots[0] + onehots[1]).astype(BF16), preferred_element_type=F32)
    sel_rows = iota((64, 48), 0)
    sel_expert = 2 * (sel_rows // CAP) + half
    sel_slot = sel_rows % CAP
    col_ids = iota((48, 64), 1)
    col_expert = 2 * (col_ids // CAP) + half
    col_slot = col_ids % CAP
    dispatch = jnp.zeros((64, 48), F32)
    picks = []
    for c in range(2):
        pos_col = jnp.sum(onehots[c] * counts, axis=1, keepdims=True).astype(jnp.int32)
        id_col = ids[:, c : c + 1]
        pos_row = jnp.sum(jnp.where(eye, pos_col, 0), axis=0, keepdims=True)
        id_row = jnp.sum(jnp.where(eye, id_col, 0), axis=0, keepdims=True)
        dispatch = dispatch + ((id_row == sel_expert) & (pos_row == sel_slot)).astype(F32)
        picks.append(((id_col == col_expert) & (pos_col == col_slot)).astype(F32))
    dispatch = dispatch.astype(BF16)

    for r in range(12):
        for which in range(2):
            sinks[which, 4 * r : 4 * r + 4, :] = sink_ref[which, r].astype(F32)

    lane48 = iota((48, 128), 1)

    def tiles_of(group):
        b0, b1, b2, b3 = (qkv_in[4 * group + k].astype(F32) for k in range(4))
        r1 = pltpu.roll(b1, 96, 1)
        r2 = pltpu.roll(b2, 64, 1)
        r3 = pltpu.roll(b3, 32, 1)
        return (
            jnp.where(lane48 < 96, b0, r1),
            jnp.where(lane48 < 64, r1, r2),
            jnp.where(lane48 < 32, r2, r3),
        )

    wait_bytes(qkv_in.at[pl.ds(0, seq_count - 1)], recv_sem.at[0])
    tiles = []
    for group in range(3):
        for at, tile in enumerate(tiles_of(group)):
            tiles.append(tile)
            qkv[3 * group + at] = tile
    sub6 = iota((6, 8, 128), 1)
    lane6 = iota((6, 8, 128), 2)
    diag6 = (sub6 < 4) == (lane6 < 64)
    zero6 = jnp.zeros((6, 8, 128), F32)
    for u in range(4):
        tops = []
        for tile in (tiles[2 * u], tiles[2 * u + 1]):
            v = tile.reshape(6, 8, 128)
            w = pltpu.roll(v, 4, 1)
            even = jnp.where(diag6, jnp.where(sub6 < 4, v, w), 0.0)
            odd = jnp.where(diag6, jnp.where(sub6 < 4, w, v), 0.0)
            tops.append((even, odd))
        for parity in range(2):
            upper = jnp.concatenate([tops[0][parity], zero6], axis=2)
            lower = jnp.concatenate([zero6, tops[1][parity]], axis=2)
            q4[:, parity, u] = jnp.concatenate([upper, lower], axis=1).astype(BF16)

    for part in range(3):
        for which in range(2):
            pltpu.make_async_copy(
                cache_hbm.at[which, pl.ds(4 * part, 4)],
                kv.at[which, pl.ds(4 * part, 4)],
                kv_sem.at[which, part],
            ).wait()

    sub8 = iota((8, 8, 128), 1)
    lane8 = iota((8, 8, 128), 2)
    lane_in = lane8 % 64
    step_id = iota((8, 128), 0) % STEPS
    slot_id = s * 128 + iota((8, 128), 1)

    def merge(a, b):
        ar = pltpu.roll(a, 4, 1)
        br = pltpu.roll(b, 4, 1)
        return jnp.where(
            sub8 < 4, jnp.where(lane8 < 64, a, ar), jnp.where(lane8 < 64, br, b)
        )

    def attend(pair, parity):
        r = 2 * pair + parity
        scores = []
        for u in range(4):
            scores.append(
                lax.dot_general(
                    q4[pair, parity, u],
                    kv[0, r, :, 256 * u : 256 * u + 256],
                    LAST,
                    preferred_element_type=F32,
                )
            )
        score = jnp.concatenate(scores, axis=0).reshape(8, 8, 128) * (HD ** (-0.5))
        held = lengths_ref[r] - SINKS
        age = (slot_id - held) & (WIN - 1)
        live = ((slot_id < jnp.minimum(WIN, held)) & (age > step_id))[None]
        peak = jnp.max(jnp.where(live, score, MASKED), axis=-1, keepdims=True)
        weight = jnp.where(live, jnp.exp(score - peak), 0.0)
        total = jnp.sum(weight, axis=-1, keepdims=True)
        rounded = weight.reshape(64, 128).astype(BF16)
        values = []
        for u in range(4):
            mixed = jnp.dot(
                rounded[16 * u : 16 * u + 16],
                kv[1, r, :, 256 * u : 256 * u + 256],
                preferred_element_type=F32,
            )
            values.append(mixed[0:8, 0:128])
            values.append(mixed[8:16, 128:256])
        value = jnp.concatenate(values, axis=0).reshape(8, 8, 128)
        peak = jnp.broadcast_to(peak, (8, 8, 128))
        total = jnp.broadcast_to(total, (8, 8, 128))
        p_hi = peak.astype(BF16).astype(F32)
        p_mid = (peak - p_hi).astype(BF16).astype(F32)
        p_low = peak - p_hi - p_mid
        t_hi = total.astype(BF16).astype(F32)
        t_low = total - t_hi
        stat = jnp.where(
            lane_in == 0,
            p_hi,
            jnp.where(
                lane_in == 1,
                p_mid,
                jnp.where(
                    lane_in == 2,
                    p_low,
                    jnp.where(lane_in == 3, t_hi, jnp.where(lane_in == 4, t_low, 0.0)),
                ),
            ),
        )
        return value, stat

    def attend_rows(group, _):
        halves = []
        for at in range(2):
            va, sa = attend(2 * group + at, 0)
            vb, sb = attend(2 * group + at, 1)
            halves.append((merge(va, vb), merge(sa, sb)))
        value = jnp.concatenate([halves[0][0], halves[1][0]], axis=1).astype(BF16)
        stat = jnp.concatenate([halves[0][1], halves[1][1]], axis=1).astype(BF16)
        part_out[group, :, 0:16, :] = value
        part_out[group, :, 16:32, :] = stat

        def send(tile, _):
            dest = 4 * tile + group

            @pl.when(dest != s)
            def _():
                rcopy(part_out.at[group, tile], part_in.at[s], 2, dest, z)

            return 0

        lax.fori_loop(0, 8, send, 0)
        return 0

    lax.fori_loop(0, 3, attend_rows, 0)

    for group in range(3, 8):
        for at, tile in enumerate(tiles_of(group)):
            qkv[3 * group + at] = tile

    wait_bytes(w_rows.at[pl.ds(0, 3)], recv_sem.at[1])

    @pl.when(rg < 3)
    def _():
        part_in[s] = part_out[rg, t]
        rows = pl.ds(pl.multiple_of(16 * rg, 16), 16)
        lanes = pl.ds(pl.multiple_of(128 * t, 128), 128)
        q_own = qkv[t, rows, :]
        k_own = qkv[8 + t, rows, :].astype(BF16)
        v_own = qkv[16 + t, rows, :].astype(BF16)
        k_sink = sinks[0, rows, lanes].astype(BF16)
        v_sink = sinks[1, rows, lanes].astype(BF16)
        rep_row = iota((64, 16), 0)
        rep_col = iota((64, 16), 1)
        repeat = (
            ((rep_row % 16) // 4 == rep_col // 4) & (rep_row // 16 == rep_col % 4)
        ).astype(F32).astype(BF16)
        keys = jnp.concatenate(
            [
                jnp.dot(repeat, k_sink, preferred_element_type=F32),
                jnp.dot(repeat, k_own, preferred_element_type=F32),
            ],
            axis=0,
        ).reshape(8, 16, 128)
        vals = jnp.concatenate(
            [
                jnp.dot(repeat, v_sink, preferred_element_type=F32),
                jnp.dot(repeat, v_own, preferred_element_type=F32),
            ],
            axis=0,
        ).reshape(8, 16, 128)
        prod = (q_own[None] * keys).reshape(128, 128)
        prod_hi = prod.astype(BF16)
        prod_low = (prod - prod_hi.astype(F32)).astype(BF16)
        same_half = (
            (iota((128, 128), 0) < 64) == (iota((128, 128), 1) < 64)
        ).astype(F32).astype(BF16)
        score = (
            jnp.dot(prod_hi, same_half, preferred_element_type=F32)
            + jnp.dot(prod_low, same_half, preferred_element_type=F32)
        ).reshape(8, 16, 128) * (HD ** (-0.5))
        key_id = iota((8, 16, 128), 0)
        row_step = iota((8, 16, 128), 1) % STEPS
        live = (key_id < SINKS) | (key_id - SINKS <= row_step)
        near_peak = jnp.max(jnp.where(live, score, MASKED), axis=0)
        weight = jnp.where(live, jnp.exp(score - near_peak[None]), 0.0)
        near_total = jnp.sum(weight, axis=0)
        near_value = jnp.sum(weight.astype(BF16).astype(F32) * vals, axis=0)

        wait_bytes(part_in.at[pl.ds(0, seq_count - 1)], recv_sem.at[2])
        spread_row = iota((128, 256), 0)
        spread_col = iota((128, 256), 1)
        kk = spread_row % 64
        wanted = jnp.where(spread_col < 128, (kk < 3).astype(F32), ((kk == 3) | (kk == 4)).astype(F32))
        spread = jnp.where(
            (spread_row < 64) == (spread_col % 128 < 64), wanted, 0.0
        ).astype(BF16)
        stats = jnp.dot(
            part_in[:, 16:32, :].reshape(seq_count * 16, 128), spread, preferred_element_type=F32
        ).reshape(seq_count, 16, 256)
        peaks = stats[:, :, 0:128]
        totals = stats[:, :, 128:256]
        overall = jnp.maximum(jnp.max(peaks, axis=0), near_peak)
        factor = jnp.exp(peaks - overall[None])
        near_factor = jnp.exp(near_peak - overall)
        total = jnp.sum(factor * totals, axis=0) + near_factor * near_total
        value = (
            jnp.sum(factor * part_in[:, 0:16, :].astype(F32), axis=0) + near_factor * near_value
        )
        att_in[t] = (value / total).astype(BF16)

        def send_att(k, _):
            rcopy(att_in.at[t], att_in.at[t], 3, 4 * lax.rem(t + k, 8) + rg, z)
            return 0

        lax.fori_loop(1, 8, send_att, 0)
        wait_bytes(att_in.at[pl.ds(0, 7)], recv_sem.at[3])
        attended = jnp.concatenate([att_in[k] for k in range(8)], axis=1)
        weights = w_rows[...].reshape(128, 1024)
        proj_in[8 * rg + t] = lax.dot_general(
            attended, weights, LAST, preferred_element_type=F32
        ).astype(BF16)
        to_plane(proj_in.at[8 * rg + t], proj_in.at[8 * rg + t], 4)
        wait_bytes(proj_in.at[pl.ds(0, 23)], recv_sem.at[4])

    @pl.when(rg == 3)
    def _():
        wait_bytes(proj_in, recv_sem.at[4])

    projected = jnp.concatenate(
        [
            jnp.concatenate([proj_in[8 * g + k] for k in range(8)], axis=1)
            for g in range(3)
        ],
        axis=0,
    )
    residual = x_tok[...] + projected.astype(F32)
    x_tok[...] = residual
    inverse = lax.rsqrt(jnp.mean(residual * residual, axis=-1, keepdims=True) + EPSILON)
    normed = (residual * inverse * moe_gain_ref[...]).astype(BF16)
    buffer = jnp.dot(dispatch, normed, preferred_element_type=F32)
    disp_out[...] = buffer.reshape(8, 8, 1024).astype(BF16)

    def send_rows(k, _):
        dest = lax.rem(z + k, group_count)
        rcopy(disp_out.at[dest], disp_in.at[z], 5, s, dest)
        return 0

    lax.fori_loop(1, group_count, send_rows, 0)
    disp_in[z] = disp_out[z]

    logits = jnp.dot(normed, router_ref[...], preferred_element_type=F32)
    gates = jnp.zeros((48, 64), F32)
    for c in range(2):
        logit = jnp.sum(onehots[c] * logits, axis=1, keepdims=True)
        gates = gates + picks[c] * jax.nn.sigmoid(logit)
    gates_hi = gates.astype(BF16)
    gates_low = (gates - gates_hi.astype(F32)).astype(BF16)

    pltpu.make_async_copy(in_hbm.at[:, 0], win, wt_sem.at[0]).wait()
    pltpu.make_async_copy(down_hbm.at[0], down, wt_sem.at[1]).wait()
    wait_bytes(disp_in.at[pl.ds(0, group_count - 1)], recv_sem.at[5])
    rows_in = disp_in[...].astype(F32).reshape(64, 1024).astype(BF16)
    gate_part = lax.dot_general(rows_in, win[0], LAST, preferred_element_type=F32)
    up_part = lax.dot_general(rows_in, win[1], LAST, preferred_element_type=F32)
    hidden = (jax.nn.gelu(gate_part, approximate=True) * up_part).astype(BF16)
    partial = jnp.dot(hidden, down[...], preferred_element_type=F32).astype(BF16)
    for g in range(2):
        for k in range(8):
            exp_out[8 * g + k] = partial[32 * g : 32 * g + 32, 128 * k : 128 * k + 128]

    def send_exp(k, _):
        dest = lax.rem(owner16 + k, 16)
        rcopy(exp_out.at[dest], exp_in.at[owner16], 6, 16 * half + dest, z)
        return 0

    lax.fori_loop(1, 16, send_exp, 0)
    exp_in[owner16] = exp_out[owner16]
    wait_bytes(exp_in.at[pl.ds(0, 15)], recv_sem.at[6])
    summed = jnp.sum(exp_in[...].astype(F32), axis=0)
    back_out[...] = summed.reshape(4, 8, 128).astype(BF16)

    def send_back(k, _):
        dest = 4 * gh + k

        @pl.when(dest != z)
        def _():
            rcopy(back_out.at[k], back_in.at[z], 7, s, dest)

        return 0

    lax.fori_loop(0, 4, send_back, 0)
    here = gh == z // 4

    @pl.when(here)
    def _():
        back_in[z] = back_out[lax.rem(z, 4)]
        wait_bytes(back_in.at[pl.ds(0, group_count - 1)], recv_sem.at[7])
        returned = back_in[...].astype(F32).reshape(64, 128).astype(BF16)
        fin_in[owner8] = (
            jnp.dot(gates_hi, returned, preferred_element_type=F32)
            + jnp.dot(gates_low, returned, preferred_element_type=F32)
        ).astype(BF16)
        to_plane(fin_in.at[owner8], fin_in.at[owner8], 8)
        wait_bytes(fin_in.at[pl.ds(0, 15)], recv_sem.at[8])

    @pl.when(jnp.logical_not(here))
    def _():
        wait_bytes(fin_in, recv_sem.at[8])

    for k in range(8):
        lanes = slice(128 * k, 128 * k + 128)
        out_ref[:, lanes] = (
            x_tok[:, lanes] + (fin_in[k].astype(F32) + fin_in[8 + k].astype(F32))
        ).astype(BF16)

    wait_bytes(qkv_in.at[pl.ds(0, seq_count - 1)], send_sem.at[0])
    wait_bytes(w_rows.at[pl.ds(0, 3)], send_sem.at[1])

    @pl.when(rg < 3)
    def _():
        wait_bytes(part_in.at[pl.ds(0, 23)], send_sem.at[2])
        wait_bytes(att_in.at[pl.ds(0, 7)], send_sem.at[3])
        wait_bytes(part_in.at[pl.ds(0, 31), pl.ds(0, 16)], send_sem.at[4])

    @pl.when(rg == 3)
    def _():
        wait_bytes(part_in.at[pl.ds(0, 24)], send_sem.at[2])

    wait_bytes(disp_in.at[pl.ds(0, group_count - 1)], send_sem.at[5])
    wait_bytes(exp_in.at[pl.ds(0, 15)], send_sem.at[6])

    @pl.when(here)
    def _():
        wait_bytes(back_out.at[pl.ds(0, 3)], send_sem.at[7])
        wait_bytes(qkv_in.at[pl.ds(0, seq_count - 1)], send_sem.at[8])

    @pl.when(jnp.logical_not(here))
    def _():
        wait_bytes(back_out, send_sem.at[7])


def solution(mesh):
    seq_count = mesh.shape["seq"]
    group_count = mesh.shape["exp"]
    vmem = pl.BlockSpec(memory_space=pltpu.VMEM)
    hbm = pl.BlockSpec(memory_space=pl.ANY)
    smem = pl.BlockSpec(memory_space=pltpu.SMEM)

    def body(
        tokens,
        attn_gain,
        w_qkv,
        window_cache,
        sink_cache,
        lengths,
        w_out,
        moe_gain,
        router,
        expert_ids,
        slot_order,
        expert_in,
        expert_down,
    ):
        out = pl.pallas_call(
            functools.partial(layer_kernel, seq_count, group_count),
            out_shape=jax.ShapeDtypeStruct((48, 1024), BF16),
            in_specs=[vmem, vmem, vmem, hbm, vmem, smem, vmem, vmem, vmem, vmem, vmem, hbm, hbm],
            out_specs=vmem,
            scratch_shapes=[
                pltpu.VMEM((2, 12, 128, 1024), BF16),
                pltpu.VMEM((2, 176, 1024), BF16),
                pltpu.VMEM((176, 1024), BF16),
                pltpu.VMEM((48, 1024), F32),
                pltpu.VMEM((48, 2), jnp.int32),
                pltpu.VMEM((48, 128), BF16),
                pltpu.VMEM((32, 48, 128), BF16),
                pltpu.VMEM((24, 48, 128), F32),
                pltpu.VMEM((6, 2, 4, 16, 256), BF16),
                pltpu.VMEM((3, 8, 32, 128), BF16),
                pltpu.VMEM((32, 32, 128), BF16),
                pltpu.VMEM((2, 48, 1024), F32),
                pltpu.VMEM((8, 16, 128), BF16),
                pltpu.VMEM((4, 32, 1024), BF16),
                pltpu.VMEM((24, 16, 128), BF16),
                pltpu.VMEM((8, 8, 1024), BF16),
                pltpu.VMEM((8, 8, 1024), BF16),
                pltpu.VMEM((16, 32, 128), BF16),
                pltpu.VMEM((16, 32, 128), BF16),
                pltpu.VMEM((4, 8, 128), BF16),
                pltpu.VMEM((8, 8, 128), BF16),
                pltpu.VMEM((16, 48, 128), BF16),
                pltpu.SemaphoreType.DMA((2, 3)),
                pltpu.SemaphoreType.DMA((2,)),
                pltpu.SemaphoreType.DMA((1,)),
                pltpu.SemaphoreType.DMA((9,)),
                pltpu.SemaphoreType.DMA((9,)),
            ],
            compiler_params=pltpu.CompilerParams(
                collective_id=0, has_side_effects=True, vmem_limit_bytes=48 * 1024 * 1024
            ),
            name="layer",
        )(
            tokens,
            attn_gain.reshape(1, -1),
            w_qkv,
            window_cache,
            sink_cache,
            lengths,
            w_out,
            moe_gain.reshape(1, -1),
            router,
            expert_ids,
            slot_order,
            expert_in,
            expert_down,
        )
        return out.reshape(tokens.shape)

    in_specs = (
        P("exp", None, None),
        P(),
        P("seq", None),
        P(None, "exp", "seq", None),
        P(None, "exp", None, None),
        P("exp"),
        P("seq", None),
        P(),
        P(),
        P("exp", None, None),
        P("exp", None),
        P(None, "exp", "seq", None),
        P("exp", "seq", None),
    )
    out_specs = P("exp", None, None)
    return jax.shard_map(body, mesh=mesh, in_specs=in_specs, out_specs=out_specs, check_vma=False)
```

time: 497 us -> 71.8 us (0.14)
  blocking collectives: 299 us -> 0 us
  waiting for transfers between devices: 130 us -> 0 us
  Pallas kernels: 0 us -> 60.6 us
  starting transfers between devices: 15 us -> 0 us
  between operations: 13.8 us -> 0.03 us
  local copies, waits for them, and re-layouts: 22.1 us -> 10.8 us
  matrix products: 10.1 us -> 0 us
  other arithmetic: 6.1 us -> 0 us
    psum x1 -> x0, blocking collectives: 124 us -> none  [body(): lax.psum((weight_sum * factor).astype(jnp.bfloat16), 'seq')]
    pmax x1 -> x0, blocking collectives: 121 us -> none  [body(): overall = lax.pmax(peak_score, 'seq')]
    psum x2 -> x0, waiting for transfers between devices: 107 us -> none  [the longest x1 107 us: body(): summed = lax.psum(expert_part.astype(jnp.bfloat16), 'seq')]
    pallas_call x0 -> x1, Pallas kernels: none -> 60.6 us  [body(): pl.pallas_call(functools.partial(layer_kernel, seq_count, group_count), o...]
    all_gather x2 -> x0, blocking collectives: 54.1 us -> none  [the longest x1 27.6 us: body(): projected = lax.all_gather(local_proj, 'seq', axis=1, tiled=True)]
    all_to_all x2 -> x0, waiting for transfers between devices: 22.6 us -> none  [the longest x1 12.2 us: body(): lax.all_to_all(buffer, 'exp', split_axis=0, concat_axis=0, tiled=True)]
    slice x5 -> x0, local copies, waits for them, and re-layouts: 16.3 us -> none  [the longest x2 11.3 us: body(): cache_values = window_cache[1].reshape(requests, slot_span, HEADS, HD)]
    all_to_all x2 -> x0, starting transfers between devices: 14.9 us -> none  [the longest x1 8.2 us: body(): lax.all_to_all(buffer, 'exp', split_axis=0, concat_axis=0, tiled=True)]
  transfers between devices with their start and end apart: 4 -> 0, of which waited for: 3 -> 0; matrix products, arithmetic and copies ran while one was open for 0% -> 0% of each run, Pallas kernels for 0% -> 0%
where the time goes in v1:
time: 71.8 us; the launch traced here: 71.4 us
  Pallas kernels  60.6 us (84%)
  local copies, waits for them, and re-layouts  10.8 us (15%)
    pallas_call x1, Pallas kernels, body(): pl.pallas_call(functools.partial(layer_kernel, seq_count, group_count), o...  60.6 us
    unnamed x22, local copies, waits for them, and re-layouts  10.1 us

profile of v1, /device:TPU:1, one launch (start us, length us, event | category | flops | bytes accessed | tf_op | source)
XLA Modules:
  0.0 71.4 jit_solution(12521132442370721373)
XLA Ops:
  0.0 0.8 %copy.15.ids_ref = s32[12,4,2]{2,1,0:T(4,128)S(1)} copy(s32[12,4,2]{0,2,1:T(2,128)} %param.22) | data formatting | bytes 768 | tf_op args[9]
  0.8 0.9 %copy.14.router_ref = bf16[1024,16]{1,0:T(8,128)(2,1)S(1)} copy(bf16[1024,16]{0,1:T(8,128)(2,1)} %param.21) | data formatting | bytes 65536 | tf_op args[8]
  1.7 0.0 copy-start
  1.7 1.1 %copy-done = bf16[2,1,176,1024]{3,2,1,0:T(8,128)(2,1)S(1)} copy-done((bf16[2,1,176,1024]{3,2,1,0:T(8,128)(2,1)S(1)}, bf16[2,1,176,1024]{3,2,1,0:T(8,128)(2,1)}, u32[]{:S(2)}) %copy-start) | copy-done | bytes 720920
  2.8 0.0 copy-start.1
  2.8 1.0 %copy-done.1 = bf16[1,176,1024]{2,1,0:T(8,128)(2,1)S(1)} copy-done((bf16[1,176,1024]{2,1,0:T(8,128)(2,1)S(1)}, bf16[1,176,1024]{2,1,0:T(8,128)(2,1)}, u32[]{:S(2)}) %copy-start.1) | copy-done | bytes 360472
  3.8 0.0 copy-start.2
  3.8 0.9 %copy-done.2 = bf16[96,1024]{1,0:T(8,128)(2,1)S(1)} copy-done((bf16[96,1024]{1,0:T(8,128)(2,1)S(1)}, bf16[96,1024]{1,0:T(8,128)(2,1)}, u32[]{:S(2)}) %copy-start.2) | copy-done | bytes 196632
  4.8 0.0 copy-start.3
  4.8 0.9 %copy-done.3 = bf16[2,12,4,1024]{3,2,1,0:T(4,128)(2,1)S(1)} copy-done((bf16[2,12,4,1024]{3,2,1,0:T(4,128)(2,1)S(1)}, bf16[2,12,4,1024]{3,2,1,0:T(4,128)(2,1)}, u32[]{:S(2)}) %copy-start.3) | copy-done | bytes 196632
  5.7 0.0 copy-start.4
  5.7 0.9 %copy-done.4 = bf16[12,4,1024]{2,1,0:T(4,128)(2,1)S(1)} copy-done((bf16[12,4,1024]{2,1,0:T(4,128)(2,1)S(1)}, bf16[12,4,1024]{2,1,0:T(4,128)(2,1)}, u32[]{:S(2)}) %copy-start.4) | copy-done | bytes 98328
  6.6 0.0 copy-start.5
  6.6 0.8 %copy-done.5 = bf16[32,1024]{1,0:T(8,128)(2,1)S(1)} copy-done((bf16[32,1024]{1,0:T(8,128)(2,1)S(1)}, bf16[32,1024]{1,0:T(8,128)(2,1)}, u32[]{:S(2)}) %copy-start.5) | copy-done | bytes 65560
  7.4 0.0 copy-start.6
  7.4 0.7 copy-done.6
  8.1 0.0 copy-start.7
  8.1 0.7 copy-done.7
  8.8 0.0 copy-start.8
  8.8 0.7 copy-done.8
  9.4 0.0 copy-start.9
  9.4 0.7 copy-done.9
  10.1 60.6 %layer.1 = bf16[48,1024]{1,0:T(8,128)(2,1)S(1)} custom-call(bf16[12,4,1024]{2,1,0:T(4,128)(2,1)S(1)} %copy-done.4, f32[1,1024]{1,0:T(1,128)S(1)} %bitcast.2, bf16[96,1024]{1,0:T(8,128)(2,1)S(1)} %copy-done.2, bf16[2,12,128,1024]{3,2,1,0:T(8,128)(2,1)} %cache_hbm.1, bf16[2,12,4,1024]{3,2,1,0:T(4,128)(2,1)S(1)} %copy-done.3, s32[12]{0:T(128)S(1)} %copy-done.8, ...), custom_call_target="tpu_custom_call" | custom-call | tf_op jit(solution)/shard_map/layer/pallas_call | solution.py:541
  70.7 0.7 reshape.11
Async XLA Ops:
  1.7 1.1 %copy-start = (bf16[2,1,176,1024]{3,2,1,0:T(8,128)(2,1)S(1)}, bf16[2,1,176,1024]{3,2,1,0:T(8,128)(2,1)}, u32[]{:S(2)}) copy-start(bf16[2,1,176,1024]{3,2,1,0:T(8,128)(2,1)} %in_hbm.1) | copy-start | bytes 2162692
  2.8 1.0 %copy-start.1 = (bf16[1,176,1024]{2,1,0:T(8,128)(2,1)S(1)}, bf16[1,176,1024]{2,1,0:T(8,128)(2,1)}, u32[]{:S(2)}) copy-start(bf16[1,176,1024]{2,1,0:T(8,128)(2,1)} %down_hbm.1) | copy-start | bytes 1081348
  3.8 0.9 %copy-start.2 = (bf16[96,1024]{1,0:T(8,128)(2,1)S(1)}, bf16[96,1024]{1,0:T(8,128)(2,1)}, u32[]{:S(2)}) copy-start(bf16[96,1024]{1,0:T(8,128)(2,1)} %w_qkv_ref.1) | copy-start | bytes 589828
  4.8 0.9 %copy-start.3 = (bf16[2,12,4,1024]{3,2,1,0:T(4,128)(2,1)S(1)}, bf16[2,12,4,1024]{3,2,1,0:T(4,128)(2,1)}, u32[]{:S(2)}) copy-start(bf16[2,12,4,1024]{3,2,1,0:T(4,128)(2,1)} %sink_ref.1) | copy-start | bytes 589828
  5.7 0.9 %copy-start.4 = (bf16[12,4,1024]{2,1,0:T(4,128)(2,1)S(1)}, bf16[12,4,1024]{2,1,0:T(4,128)(2,1)}, u32[]{:S(2)}) copy-start(bf16[12,4,1024]{2,1,0:T(4,128)(2,1)} %tokens_ref.1) | copy-start | bytes 294916
  6.6 0.8 %copy-start.5 = (bf16[32,1024]{1,0:T(8,128)(2,1)S(1)}, bf16[32,1024]{1,0:T(8,128)(2,1)}, u32[]{:S(2)}) copy-start(bf16[32,1024]{1,0:T(8,128)(2,1)} %w_out_ref.1) | copy-start | bytes 196612
  7.4 0.7 copy-start.6
  8.1 0.7 copy-start.7
  8.8 0.7 copy-start.8
  9.4 0.7 copy-start.9

commit v2 on v1

--- a/solution.py
+++ b/solution.py
@@ -16,6 +16,7 @@
 STEPS = 4
 EPSILON = 1e-06
 MASKED = -1e30
+QUERY_BLOCKS = 11
 MESH = pl.DeviceIdType.MESH
 F32 = jnp.float32
 BF16 = jnp.bfloat16
@@ -33,10 +34,23 @@
 def layer_kernel(
     seq_count,
     group_count,
+    tokens_hbm,
+    attn_gain_hbm,
+    w_qkv_hbm,
+    cache_hbm,
+    sink_hbm,
+    lengths_hbm,
+    w_out_hbm,
+    moe_gain_hbm,
+    router_hbm,
+    ids_hbm,
+    order_hbm,
+    in_hbm,
+    down_hbm,
+    out_ref,
     tokens_ref,
     attn_gain_ref,
     w_qkv_ref,
-    cache_hbm,
     sink_ref,
     lengths_ref,
     w_out_ref,
@@ -44,17 +58,14 @@
     router_ref,
     ids_ref,
     order_ref,
-    in_hbm,
-    down_hbm,
-    out_ref,
     kv,
     win,
     down,
     x_tok,
-    idcol,
     mix,
     qkv_in,
     qkv,
+    near,
     q4,
     part_out,
     part_in,
@@ -69,20 +80,46 @@
     back_out,
     back_in,
     fin_in,
+    mix_send,
+    mix_recv,
     kv_sem,
     wt_sem,
-    loc_sem,
+    arg_sem,
     send_sem,
     recv_sem,
 ):
     s = lax.axis_index("seq")
     z = lax.axis_index("exp")
-    t = s // 4
-    rg = lax.rem(s, 4)
+    col = s // 8
+    rg = lax.rem(s // 2, 4)
+    core = lax.rem(s, 2)
+    t = 2 * col + core
     half = s // 16
     owner16 = lax.rem(s, 16)
-    gh = owner16 // 8
-    owner8 = 8 * half + lax.rem(s, 8)
+    owner = rg < 3
+    own_rows = core == rg // 2
+
+    def holder(tile, group):
+        return 8 * (tile // 2) + 2 * group + lax.rem(tile, 2)
+
+    small = (
+        (tokens_hbm, tokens_ref),
+        (w_qkv_hbm, w_qkv_ref),
+        (attn_gain_hbm, attn_gain_ref),
+        (w_out_hbm, w_out_ref),
+        (ids_hbm, ids_ref),
+        (order_hbm, order_ref),
+        (sink_hbm, sink_ref),
+        (lengths_hbm, lengths_ref),
+        (moe_gain_hbm, moe_gain_ref),
+        (router_hbm, router_ref),
+    )
+
+    def fetch(at):
+        return pltpu.make_async_copy(small[at][0], small[at][1], arg_sem.at[at])
+
+    for at in range(len(small)):
+        fetch(at).start()
 
     barrier = pltpu.get_barrier_semaphore()
 
@@ -128,6 +165,8 @@
 
         lax.fori_loop(1, seq_count, send, 0)
 
+    for at in range(3):
+        fetch(at).wait()
     for r in range(12):
         x_tok[4 * r : 4 * r + 4, :] = tokens_ref[r].astype(F32)
     x = x_tok[...]
@@ -137,23 +176,76 @@
     mix[...] = jnp.concatenate([own_mix, jnp.zeros((48, 32), F32)], axis=1).astype(BF16)
 
     pl.semaphore_wait(barrier, seq_count - 1 + group_count - 1)
-    to_plane(mix, qkv_in.at[s], 0)
+
+    def send_mix(at, dest):
+        return pltpu.make_async_remote_copy(
+            src_ref=mix,
+            dst_ref=qkv_in.at[s],
+            send_sem=mix_send.at[at],
+            recv_sem=mix_recv.at[s],
+            device_id=(dest, z),
+            device_id_type=MESH,
+        )
+
+    has_query = s < QUERY_BLOCKS
+    first_tile = (96 * s) // 128
+    last_tile = (96 * s + 95) // 128
+
+    @pl.when(has_query)
+    def _():
+        def send(k, _):
+            send_mix(0, lax.rem(s + k, seq_count)).start()
+            return 0
+
+        lax.fori_loop(1, seq_count, send, 0)
+
+    def each_owner(act):
+        for group in range(3):
+            for at, tile in enumerate((first_tile, last_tile)):
+                dest = holder(lax.rem(tile, 8), group)
+                go = jnp.logical_not(has_query) & (dest != s)
+                if at == 1:
+                    go = go & (first_tile != last_tile)
+
+                @pl.when(go)
+                def _():
+                    act(send_mix(1 + 2 * group + at, dest))
+
+    each_owner(lambda copy: copy.start())
     qkv_in[s] = mix[...]
-    w_rows[rg] = w_out_ref[...]
-    for k in range(1, 4):
-        rcopy(w_out_ref, w_rows.at[rg], 1, 4 * t + lax.rem(rg + k, 4), z)
-
-    for r in range(12):
-        idcol[4 * r : 4 * r + 4, :] = ids_ref[r]
+    fetch(3).wait()
+
+    w_at = 2 * lax.rem(rg, 2) + core
+
+    @pl.when(owner & own_rows)
+    def _():
+        w_rows[w_at] = w_out_ref[...]
+
+    for group in range(3):
+        w_dest = 8 * col + 2 * group + rg // 2
+
+        @pl.when(w_dest != s)
+        def _():
+            rcopy(w_out_ref, w_rows.at[w_at], 1, w_dest, z)
+
+    for at in range(4, 10):
+        fetch(at).wait()
     eye = iota((48, 48), 0) == iota((48, 48), 1)
     prio_row = order_ref[...]
     prio_col = jnp.sum(jnp.where(eye, prio_row, 0), axis=1, keepdims=True)
     earlier = (prio_row < prio_col).astype(F32).astype(BF16)
     expert_lane = iota((48, EXPERTS), 1)
-    ids = idcol[...]
+    id_row_of = iota((48, 12), 0)
+    id_lane = iota((48, 12), 1)
+    id_cols = []
     onehots = []
     for c in range(2):
-        onehots.append((expert_lane == ids[:, c : c + 1]).astype(F32))
+        spread_ids = jnp.zeros((48, 12), jnp.int32)
+        for step in range(STEPS):
+            wanted = (id_row_of // STEPS == id_lane) & (id_row_of % STEPS == step)
+            spread_ids = spread_ids + jnp.where(wanted, ids_ref[step, c : c + 1, :], 0)
+        id_cols.append(jnp.sum(spread_ids, axis=1, keepdims=True))
+        onehots.append((expert_lane == id_cols[c]).astype(F32))
     counts = jnp.dot(earlier, (onehots[0] + onehots[1]).astype(BF16), preferred_element_type=F32)
     sel_rows = iota((64, 48), 0)
     sel_expert = 2 * (sel_rows // CAP) + half
@@ -165,7 +257,7 @@
     picks = []
     for c in range(2):
         pos_col = jnp.sum(onehots[c] * counts, axis=1, keepdims=True).astype(jnp.int32)
-        id_col = ids[:, c : c + 1]
+        id_col = id_cols[c]
         pos_row = jnp.sum(jnp.where(eye, pos_col, 0), axis=0, keepdims=True)
         id_row = jnp.sum(jnp.where(eye, id_col, 0), axis=0, keepdims=True)
         dispatch = dispatch + ((id_row == sel_expert) & (pos_row == sel_slot)).astype(F32)
@@ -179,7 +271,9 @@
     lane48 = iota((48, 128), 1)
 
     def tiles_of(group):
-        b0, b1, b2, b3 = (qkv_in[4 * group + k].astype(F32) for k in range(4))
+        last = min(4 * group + 3, QUERY_BLOCKS - 1)
+        b0, b1, b2 = (qkv_in[4 * group + k].astype(F32) for k in range(3))
+        b3 = qkv_in[last].astype(F32)
         r1 = pltpu.roll(b1, 96, 1)
         r2 = pltpu.roll(b2, 64, 1)
         r3 = pltpu.roll(b3, 32, 1)
@@ -189,12 +283,22 @@
             jnp.where(lane48 < 32, r2, r3),
         )
 
-    wait_bytes(qkv_in.at[pl.ds(0, seq_count - 1)], recv_sem.at[0])
+    def wait_block(block):
+        @pl.when(block != s)
+        def _():
+            wait_bytes(qkv_in.at[block], mix_recv.at[block])
+
+    def wait_query(block, _):
+        wait_block(block)
+        return 0
+
+    lax.fori_loop(0, QUERY_BLOCKS, wait_query, 0)
     tiles = []
     for group in range(3):
         for at, tile in enumerate(tiles_of(group)):
             tiles.append(tile)
-            qkv[3 * group + at] = tile
+            if 3 * group + at < 8:
+                qkv[3 * group + at] = tile
     sub6 = iota((6, 8, 128), 1)
     lane6 = iota((6, 8, 128), 2)
     diag6 = (sub6 < 4) == (lane6 < 64)
@@ -297,7 +401,7 @@
         part_out[group, :, 16:32, :] = stat
 
         def send(tile, _):
-            dest = 4 * tile + group
+            dest = holder(tile, group)
 
             @pl.when(dest != s)
             def _():
@@ -310,20 +414,36 @@
 
     lax.fori_loop(0, 3, attend_rows, 0)
 
-    for group in range(3, 8):
-        for at, tile in enumerate(tiles_of(group)):
-            qkv[3 * group + at] = tile
-
-    wait_bytes(w_rows.at[pl.ds(0, 3)], recv_sem.at[1])
-
-    @pl.when(rg < 3)
+    @pl.when(owner & own_rows)
+    def _():
+        wait_bytes(w_rows.at[pl.ds(0, 3)], recv_sem.at[1])
+
+    @pl.when(owner & jnp.logical_not(own_rows))
+    def _():
+        wait_bytes(w_rows, recv_sem.at[1])
+
+    @pl.when(owner)
     def _():
         part_in[s] = part_out[rg, t]
         rows = pl.ds(pl.multiple_of(16 * rg, 16), 16)
         lanes = pl.ds(pl.multiple_of(128 * t, 128), 128)
         q_own = qkv[t, rows, :]
-        k_own = qkv[8 + t, rows, :].astype(BF16)
-        v_own = qkv[16 + t, rows, :].astype(BF16)
+
+        def own_tile(tile):
+            block = (128 * tile) // 96
+            offset = 128 * tile - 96 * block
+            for b in (block, block + 1):
+
+                @pl.when(b >= QUERY_BLOCKS)
+                def _():
+                    wait_block(b)
+
+            low = pltpu.roll(qkv_in[block, rows, :].astype(F32), 128 - offset, 1)
+            high = pltpu.roll(qkv_in[block + 1, rows, :].astype(F32), 96 - offset, 1)
+            return jnp.where(iota((16, 128), 1) < 96 - offset, low, high).astype(BF16)
+
+        k_own = own_tile(8 + t)
+        v_own = own_tile(16 + t)
         k_sink = sinks[0, rows, lanes].astype(BF16)
         v_sink = sinks[1, rows, lanes].astype(BF16)
         rep_row = iota((64, 16), 0)
@@ -363,7 +483,15 @@
         near_total = jnp.sum(weight, axis=0)
         near_value = jnp.sum(weight.astype(BF16).astype(F32) * vals, axis=0)
 
+        near[0] = near_peak
+        near[1] = near_total
+        near[2] = near_value
         wait_bytes(part_in.at[pl.ds(0, seq_count - 1)], recv_sem.at[2])
+
+
+    @pl.when(owner)
+    def _():
+        near_peak, near_total, near_value = near[0], near[1], near[2]
         spread_row = iota((128, 256), 0)
         spread_col = iota((128, 256), 1)
         kk = spread_row % 64
@@ -386,11 +514,15 @@
         att_in[t] = (value / total).astype(BF16)
 
         def send_att(k, _):
-            rcopy(att_in.at[t], att_in.at[t], 3, 4 * lax.rem(t + k, 8) + rg, z)
+            rcopy(att_in.at[t], att_in.at[t], 3, holder(lax.rem(t + k, 8), rg), z)
             return 0
 
         lax.fori_loop(1, 8, send_att, 0)
         wait_bytes(att_in.at[pl.ds(0, 7)], recv_sem.at[3])
+
+
+    @pl.when(owner)
+    def _():
         attended = jnp.concatenate([att_in[k] for k in range(8)], axis=1)
         weights = w_rows[...].reshape(128, 1024)
         proj_in[8 * rg + t] = lax.dot_general(
@@ -402,6 +534,7 @@
     @pl.when(rg == 3)
     def _():
         wait_bytes(proj_in, recv_sem.at[4])
+
 
     projected = jnp.concatenate(
         [
@@ -414,18 +547,19 @@
     x_tok[...] = residual
     inverse = lax.rsqrt(jnp.mean(residual * residual, axis=-1, keepdims=True) + EPSILON)
     normed = (residual * inverse * moe_gain_ref[...]).astype(BF16)
-    buffer = jnp.dot(dispatch, normed, preferred_element_type=F32)
-    disp_out[...] = buffer.reshape(8, 8, 1024).astype(BF16)
+    own_half = jnp.where(core == 0, normed[:, 0:512], normed[:, 512:1024])
+    buffer = jnp.dot(dispatch, own_half, preferred_element_type=F32)
+    disp_out[...] = buffer.reshape(8, 8, 512).astype(BF16)
 
     def send_rows(k, _):
         dest = lax.rem(z + k, group_count)
-        rcopy(disp_out.at[dest], disp_in.at[z], 5, s, dest)
+        rcopy(disp_out.at[dest], disp_in.at[core, z], 5, s, dest)
         return 0
 
     lax.fori_loop(1, group_count, send_rows, 0)
-    disp_in[z] = disp_out[z]
-
-    logits = jnp.dot(normed, router_ref[...], preferred_element_type=F32)
+    disp_in[core, z] = disp_out[z]
+
+    logits = lax.dot_general(normed, router_ref[...], LAST, preferred_element_type=F32)
     gates = jnp.zeros((48, 64), F32)
     for c in range(2):
         logit = jnp.sum(onehots[c] * logits, axis=1, keepdims=True)
@@ -435,15 +569,22 @@
 
     pltpu.make_async_copy(in_hbm.at[:, 0], win, wt_sem.at[0]).wait()
     pltpu.make_async_copy(down_hbm.at[0], down, wt_sem.at[1]).wait()
-    wait_bytes(disp_in.at[pl.ds(0, group_count - 1)], recv_sem.at[5])
-    rows_in = disp_in[...].astype(F32).reshape(64, 1024).astype(BF16)
+    wait_bytes(disp_in.at[0, pl.ds(0, group_count - 1)], recv_sem.at[5])
+    rcopy(disp_in.at[core], disp_in.at[core], 9, s + 1 - 2 * core, z)
+    wait_bytes(disp_in.at[0], recv_sem.at[9])
+    rows_in = jnp.concatenate(
+        [disp_in[c].astype(F32).reshape(64, 512).astype(BF16) for c in range(2)], axis=1
+    )
     gate_part = lax.dot_general(rows_in, win[0], LAST, preferred_element_type=F32)
     up_part = lax.dot_general(rows_in, win[1], LAST, preferred_element_type=F32)
     hidden = (jax.nn.gelu(gate_part, approximate=True) * up_part).astype(BF16)
-    partial = jnp.dot(hidden, down[...], preferred_element_type=F32).astype(BF16)
-    for g in range(2):
-        for k in range(8):
-            exp_out[8 * g + k] = partial[32 * g : 32 * g + 32, 128 * k : 128 * k + 128]
+    partial = jnp.dot(hidden, down[...], preferred_element_type=F32)
+    left32 = iota((32, 128), 1) < 64
+    for k in range(8):
+        upper = partial[0:32, 128 * k : 128 * k + 128]
+        lower = partial[32:64, 128 * k : 128 * k + 128]
+        exp_out[2 * k] = jnp.where(left32, upper, pltpu.roll(lower, 64, 1)).astype(BF16)
+        exp_out[2 * k + 1] = jnp.where(left32, pltpu.roll(upper, 64, 1), lower).astype(BF16)
 
     def send_exp(k, _):
         dest = lax.rem(owner16 + k, 16)
@@ -457,71 +598,72 @@
     back_out[...] = summed.reshape(4, 8, 128).astype(BF16)
 
     def send_back(k, _):
-        dest = 4 * gh + k
-
-        @pl.when(dest != z)
-        def _():
-            rcopy(back_out.at[k], back_in.at[z], 7, s, dest)
-
+        dest = lax.rem(z + k, group_count)
+        rcopy(back_out.at[lax.rem(dest, 4)], back_in.at[z], 7, s, dest)
         return 0
 
-    lax.fori_loop(0, 4, send_back, 0)
-    here = gh == z // 4
-
-    @pl.when(here)
-    def _():
-        back_in[z] = back_out[lax.rem(z, 4)]
-        wait_bytes(back_in.at[pl.ds(0, group_count - 1)], recv_sem.at[7])
-        returned = back_in[...].astype(F32).reshape(64, 128).astype(BF16)
-        fin_in[owner8] = (
-            jnp.dot(gates_hi, returned, preferred_element_type=F32)
-            + jnp.dot(gates_low, returned, preferred_element_type=F32)
-        ).astype(BF16)
-        to_plane(fin_in.at[owner8], fin_in.at[owner8], 8)
-        wait_bytes(fin_in.at[pl.ds(0, 15)], recv_sem.at[8])
-
-    @pl.when(jnp.logical_not(here))
-    def _():
-        wait_bytes(fin_in, recv_sem.at[8])
+    lax.fori_loop(1, group_count, send_back, 0)
+    back_in[z] = back_out[lax.rem(z, 4)]
+    wait_bytes(back_in.at[pl.ds(0, group_count - 1)], recv_sem.at[7])
+    returned = back_in[...].astype(F32).reshape(64, 128).astype(BF16)
+    shared = jnp.dot(gates_hi, returned, preferred_element_type=F32) + jnp.dot(
+        gates_low, returned, preferred_element_type=F32
+    )
+    swapped = pltpu.roll(shared, 64, 1)
+    left24 = iota((24, 128), 1) < 64
+    fin_in[s] = jnp.where(
+        z < 4,
+        jnp.where(left24, shared[0:24], swapped[24:48]),
+        jnp.where(left24, swapped[0:24], shared[24:48]),
+    ).astype(BF16)
+    to_plane(fin_in.at[s], fin_in.at[s], 8)
+    wait_bytes(fin_in.at[pl.ds(0, seq_count - 1)], recv_sem.at[8])
 
     for k in range(8):
         lanes = slice(128 * k, 128 * k + 128)
-        out_ref[:, lanes] = (
-            x_tok[:, lanes] + (fin_in[k].astype(F32) + fin_in[8 + k].astype(F32))
-        ).astype(BF16)
-
-    wait_bytes(qkv_in.at[pl.ds(0, seq_count - 1)], send_sem.at[0])
-    wait_bytes(w_rows.at[pl.ds(0, 3)], send_sem.at[1])
-
-    @pl.when(rg < 3)
+        even = fin_in[2 * k].astype(F32) + fin_in[16 + 2 * k].astype(F32)
+        odd = fin_in[2 * k + 1].astype(F32) + fin_in[17 + 2 * k].astype(F32)
+        upper = jnp.where(left24, even, pltpu.roll(odd, 64, 1))
+        lower = jnp.where(left24, pltpu.roll(even, 64, 1), odd)
+        out_ref[0:24, lanes] = (x_tok[0:24, lanes] + upper).astype(BF16)
+        out_ref[24:48, lanes] = (x_tok[24:48, lanes] + lower).astype(BF16)
+
+    @pl.when(has_query)
+    def _():
+        wait_bytes(qkv_in.at[pl.ds(0, seq_count - 1)], mix_send.at[0])
+
+    each_owner(lambda copy: copy.wait_send())
+
+    @pl.when(owner & own_rows)
+    def _():
+        wait_bytes(w_rows.at[pl.ds(0, 2)], send_sem.at[1])
+
+    @pl.when(jnp.logical_not(owner & own_rows))
+    def _():
+        wait_bytes(w_rows.at[pl.ds(0, 3)], send_sem.at[1])
+
+    @pl.when(owner)
     def _():
         wait_bytes(part_in.at[pl.ds(0, 23)], send_sem.at[2])
         wait_bytes(att_in.at[pl.ds(0, 7)], send_sem.at[3])
         wait_bytes(part_in.at[pl.ds(0, 31), pl.ds(0, 16)], send_sem.at[4])
 
-    @pl.when(rg == 3)
+    @pl.when(jnp.logical_not(owner))
     def _():
         wait_bytes(part_in.at[pl.ds(0, 24)], send_sem.at[2])
 
-    wait_bytes(disp_in.at[pl.ds(0, group_count - 1)], send_sem.at[5])
+    wait_bytes(disp_in.at[0, pl.ds(0, group_count - 1)], send_sem.at[5])
+    wait_bytes(disp_in.at[0], send_sem.at[9])
     wait_bytes(exp_in.at[pl.ds(0, 15)], send_sem.at[6])
-
-    @pl.when(here)
-    def _():
-        wait_bytes(back_out.at[pl.ds(0, 3)], send_sem.at[7])
-        wait_bytes(qkv_in.at[pl.ds(0, seq_count - 1)], send_sem.at[8])
-
-    @pl.when(jnp.logical_not(here))
-    def _():
-        wait_bytes(back_out, send_sem.at[7])
+    wait_bytes(back_in.at[pl.ds(0, group_count - 1)], send_sem.at[7])
+    wait_bytes(fin_in.at[pl.ds(0, seq_count - 1)], send_sem.at[8])
 
 
 def solution(mesh):
     seq_count = mesh.shape["seq"]
     group_count = mesh.shape["exp"]
     vmem = pl.BlockSpec(memory_space=pltpu.VMEM)
-    hbm = pl.BlockSpec(memory_space=pl.ANY)
-    smem = pl.BlockSpec(memory_space=pltpu.SMEM)
+    hbm = pl.BlockSpec(memory_space=pltpu.HBM)
 
     def body(
         tokens,
@@ -541,17 +683,27 @@
         out = pl.pallas_call(
             functools.partial(layer_kernel, seq_count, group_count),
             out_shape=jax.ShapeDtypeStruct((48, 1024), BF16),
-            in_specs=[vmem, vmem, vmem, hbm, vmem, smem, vmem, vmem, vmem, vmem, vmem, hbm, hbm],
+            in_specs=[hbm] * 13,
             out_specs=vmem,
             scratch_shapes=[
+                pltpu.VMEM((12, 4, 1024), BF16),
+                pltpu.VMEM((1, 1024), F32),
+                pltpu.VMEM((96, 1024), BF16),
+                pltpu.VMEM((2, 12, 4, 1024), BF16),
+                pltpu.SMEM((12,), jnp.int32),
+                pltpu.VMEM((32, 1024), BF16),
+                pltpu.VMEM((1, 1024), F32),
+                pltpu.VMEM((16, 1024), BF16),
+                pltpu.VMEM((4, 2, 12), jnp.int32),
+                pltpu.VMEM((1, 48), jnp.int32),
                 pltpu.VMEM((2, 12, 128, 1024), BF16),
                 pltpu.VMEM((2, 176, 1024), BF16),
                 pltpu.VMEM((176, 1024), BF16),
                 pltpu.VMEM((48, 1024), F32),
-                pltpu.VMEM((48, 2), jnp.int32),
                 pltpu.VMEM((48, 128), BF16),
                 pltpu.VMEM((32, 48, 128), BF16),
-                pltpu.VMEM((24, 48, 128), F32),
+                pltpu.VMEM((8, 48, 128), F32),
+                pltpu.VMEM((3, 16, 128), F32),
                 pltpu.VMEM((6, 2, 4, 16, 256), BF16),
                 pltpu.VMEM((3, 8, 32, 128), BF16),
                 pltpu.VMEM((32, 32, 128), BF16),
@@ -559,21 +711,23 @@
                 pltpu.VMEM((8, 16, 128), BF16),
                 pltpu.VMEM((4, 32, 1024), BF16),
                 pltpu.VMEM((24, 16, 128), BF16),
-                pltpu.VMEM((8, 8, 1024), BF16),
-                pltpu.VMEM((8, 8, 1024), BF16),
+                pltpu.VMEM((8, 8, 512), BF16),
+                pltpu.VMEM((2, 8, 8, 512), BF16),
                 pltpu.VMEM((16, 32, 128), BF16),
                 pltpu.VMEM((16, 32, 128), BF16),
                 pltpu.VMEM((4, 8, 128), BF16),
                 pltpu.VMEM((8, 8, 128), BF16),
-                pltpu.VMEM((16, 48, 128), BF16),
+                pltpu.VMEM((32, 24, 128), BF16),
+                pltpu.SemaphoreType.DMA((7,)),
+                pltpu.SemaphoreType.DMA((32,)),
                 pltpu.SemaphoreType.DMA((2, 3)),
                 pltpu.SemaphoreType.DMA((2,)),
-                pltpu.SemaphoreType.DMA((1,)),
-                pltpu.SemaphoreType.DMA((9,)),
-                pltpu.SemaphoreType.DMA((9,)),
+                pltpu.SemaphoreType.DMA((10,)),
+                pltpu.SemaphoreType.DMA((10,)),
+                pltpu.SemaphoreType.DMA((10,)),
             ],
             compiler_params=pltpu.CompilerParams(
-                collective_id=0, has_side_effects=True, vmem_limit_bytes=48 * 1024 * 1024
+                collective_id=0, has_side_effects=True, vmem_limit_bytes=67043328
             ),
             name="layer",
         )(
@@ -585,8 +739,8 @@
             lengths,
             w_out,
             moe_gain.reshape(1, -1),
-            router,
-            expert_ids,
+            router.T,
+            expert_ids.transpose(1, 2, 0),
             slot_order,
             expert_in,
             expert_down,

time: 71.8 us -> 58.7 us (0.82)
  local copies, waits for them, and re-layouts: 10.8 us -> 1.58 us
  Pallas kernels: 60.6 us -> 57 us
    unnamed x22 -> x0, local copies, waits for them, and re-layouts: 10.1 us -> none
    pallas_call x1, Pallas kernels: 60.6 us -> 57 us  [body(): pl.pallas_call(functools.partial(layer_kernel, seq_count, group_count), o...]
    reshape x1, local copies, waits for them, and re-layouts: 0.68 us -> 1.58 us  [body(): return out.reshape(tokens.shape)]
where the time goes in v2:
time: 58.7 us; the launch traced here: 58.6 us
  Pallas kernels  57 us (97%)
  local copies, waits for them, and re-layouts  1.58 us (3%)
    pallas_call x1, Pallas kernels, body(): pl.pallas_call(functools.partial(layer_kernel, seq_count, group_count), o...  57 us
    reshape x1, local copies, waits for them, and re-layouts, body(): return out.reshape(tokens.shape)  1.58 us

profile of v2, /device:TPU:1, one launch (start us, length us, event | category | flops | bytes accessed | tf_op | source)
XLA Modules:
  0.0 58.6 jit_solution(15978815554165498195)
XLA Ops:
  0.0 57.0 %layer.1 = bf16[48,1024]{1,0:T(8,128)(2,1)} custom-call(bf16[12,4,1024]{2,1,0:T(4,128)(2,1)} %tokens_hbm.1, f32[1,1024]{1,0:T(1,128)} %bitcast.5, bf16[96,1024]{1,0:T(8,128)(2,1)} %w_qkv_hbm.1, bf16[2,12,128,1024]{3,2,1,0:T(8,128)(2,1)} %cache_hbm.1, bf16[2,12,4,1024]{3,2,1,0:T(4,128)(2,1)} %sink_hbm.1, s32[12]{0:T(128)} %lengths_hbm.1, ...), custom_call_target="tpu_custom_call" | custom-call | tf_op jit(solution)/shard_map/layer/pallas_call | solution.py:683
  57.0 1.6 %reshape.11 = bf16[12,4,1024]{2,1,0:T(4,128)(2,1)} reshape(bf16[48,1024]{1,0:T(8,128)(2,1)} %layer.1) | data formatting | bytes 196608 | tf_op jit(solution)/shard_map/reshape | solution.py:748

commit v3 on v2

--- a/solution.py
+++ b/solution.py
@@ -158,12 +158,21 @@
             device_id_type=MESH,
         ).start()
 
+    def ring4(at, position):
+        return lax.rem(position + ((54 >> (2 * at)) & 3), 4)
+
+    def ring8(at, position):
+        return lax.rem(position + ((0o7162534 >> (3 * at)) & 7), group_count)
+
+    def plane_peer(k):
+        return 8 * ring4(k // 8, col) + 2 * ring4((k // 2) & 3, rg) + lax.rem(core + 1 + k, 2)
+
     def to_plane(src, dst, stage):
         def send(k, _):
-            rcopy(src, dst, stage, lax.rem(s + k, seq_count), z)
+            rcopy(src, dst, stage, plane_peer(k), z)
             return 0
 
-        lax.fori_loop(1, seq_count, send, 0)
+        lax.fori_loop(0, seq_count - 1, send, 0)
 
     for at in range(3):
         fetch(at).wait()
@@ -194,10 +203,10 @@
     @pl.when(has_query)
     def _():
         def send(k, _):
-            send_mix(0, lax.rem(s + k, seq_count)).start()
+            send_mix(0, plane_peer(k)).start()
             return 0
 
-        lax.fori_loop(1, seq_count, send, 0)
+        lax.fori_loop(0, seq_count - 1, send, 0)
 
     def each_owner(act):
         for group in range(3):
@@ -400,7 +409,8 @@
         part_out[group, :, 0:16, :] = value
         part_out[group, :, 16:32, :] = stat
 
-        def send(tile, _):
+        def send(k, _):
+            tile = 2 * ring4(k // 2, col) + lax.rem(core + k, 2)
             dest = holder(tile, group)
 
             @pl.when(dest != s)
@@ -514,10 +524,11 @@
         att_in[t] = (value / total).astype(BF16)
 
         def send_att(k, _):
-            rcopy(att_in.at[t], att_in.at[t], 3, holder(lax.rem(t + k, 8), rg), z)
+            tile = 2 * ring4(k // 2, col) + lax.rem(core + 1 + k, 2)
+            rcopy(att_in.at[t], att_in.at[t], 3, holder(tile, rg), z)
             return 0
 
-        lax.fori_loop(1, 8, send_att, 0)
+        lax.fori_loop(0, 7, send_att, 0)
         wait_bytes(att_in.at[pl.ds(0, 7)], recv_sem.at[3])
 
 
@@ -552,11 +563,11 @@
     disp_out[...] = buffer.reshape(8, 8, 512).astype(BF16)
 
     def send_rows(k, _):
-        dest = lax.rem(z + k, group_count)
+        dest = ring8(k, z)
         rcopy(disp_out.at[dest], disp_in.at[core, z], 5, s, dest)
         return 0
 
-    lax.fori_loop(1, group_count, send_rows, 0)
+    lax.fori_loop(0, group_count - 1, send_rows, 0)
     disp_in[core, z] = disp_out[z]
 
     logits = lax.dot_general(normed, router_ref[...], LAST, preferred_element_type=F32)
@@ -587,22 +598,22 @@
         exp_out[2 * k + 1] = jnp.where(left32, pltpu.roll(upper, 64, 1), lower).astype(BF16)
 
     def send_exp(k, _):
-        dest = lax.rem(owner16 + k, 16)
+        dest = 8 * lax.rem(col + 1 + k // 8, 2) + 2 * ring4((k // 2) & 3, rg) + lax.rem(core + 1 + k, 2)
         rcopy(exp_out.at[dest], exp_in.at[owner16], 6, 16 * half + dest, z)
         return 0
 
-    lax.fori_loop(1, 16, send_exp, 0)
+    lax.fori_loop(0, 15, send_exp, 0)
     exp_in[owner16] = exp_out[owner16]
     wait_bytes(exp_in.at[pl.ds(0, 15)], recv_sem.at[6])
     summed = jnp.sum(exp_in[...].astype(F32), axis=0)
     back_out[...] = summed.reshape(4, 8, 128).astype(BF16)
 
     def send_back(k, _):
-        dest = lax.rem(z + k, group_count)
+        dest = ring8(k, z)
         rcopy(back_out.at[lax.rem(dest, 4)], back_in.at[z], 7, s, dest)
         return 0
 
-    lax.fori_loop(1, group_count, send_back, 0)
+    lax.fori_loop(0, group_count - 1, send_back, 0)
     back_in[z] = back_out[lax.rem(z, 4)]
     wait_bytes(back_in.at[pl.ds(0, group_count - 1)], recv_sem.at[7])
     returned = back_in[...].astype(F32).reshape(64, 128).astype(BF16)
@@ -680,6 +691,9 @@
         expert_in,
         expert_down,
     ):
+        def pin(value):
+            return pltpu.with_memory_space_constraint(value, pltpu.HBM)
+
         out = pl.pallas_call(
             functools.partial(layer_kernel, seq_count, group_count),
             out_shape=jax.ShapeDtypeStruct((48, 1024), BF16),
@@ -727,23 +741,23 @@
                 pltpu.SemaphoreType.DMA((10,)),
             ],
             compiler_params=pltpu.CompilerParams(
-                collective_id=0, has_side_effects=True, vmem_limit_bytes=67043328
+                collective_id=0, has_side_effects=True, vmem_limit_bytes=48 * 1024 * 1024
             ),
             name="layer",
         )(
-            tokens,
-            attn_gain.reshape(1, -1),
-            w_qkv,
-            window_cache,
-            sink_cache,
-            lengths,
-            w_out,
-            moe_gain.reshape(1, -1),
-            router.T,
-            expert_ids.transpose(1, 2, 0),
-            slot_order,
-            expert_in,
-            expert_down,
+            pin(tokens),
+            pin(attn_gain.reshape(1, -1)),
+            pin(w_qkv),
+            pin(window_cache),
+            pin(sink_cache),
+            pin(lengths),
+            pin(w_out),
+            pin(moe_gain.reshape(1, -1)),
+            pin(router.T),
+            pin(expert_ids.transpose(1, 2, 0)),
+            pin(slot_order),
+            pin(expert_in),
+            pin(expert_down),
         )
         return out.reshape(tokens.shape)
 

time: 58.7 us -> 56.3 us (0.959)
  Pallas kernels: 57 us -> 55.5 us
  local copies, waits for them, and re-layouts: 1.58 us -> 0.68 us
    pallas_call x1, Pallas kernels: 57 us -> 55.5 us  [body(): pl.pallas_call(functools.partial(layer_kernel, seq_count, group_count), o...]
    reshape x1, local copies, waits for them, and re-layouts: 1.58 us -> 0.68 us  [body(): return out.reshape(tokens.shape)]
where the time goes in v3:
time: 56.3 us; the launch traced here: 56.2 us
  Pallas kernels  55.5 us (99%)
  local copies, waits for them, and re-layouts  0.68 us (1%)
    pallas_call x1, Pallas kernels, body(): pl.pallas_call(functools.partial(layer_kernel, seq_count, group_count), o...  55.5 us

profile of v3, /device:TPU:1, one launch (start us, length us, event | category | flops | bytes accessed | tf_op | source)
XLA Modules:
  0.0 56.2 jit_solution(3162302500886666661)
XLA Ops:
  0.0 55.5 %layer.1 = bf16[48,1024]{1,0:T(8,128)(2,1)S(1)} custom-call(bf16[12,4,1024]{2,1,0:T(4,128)(2,1)} %tokens_hbm.1, f32[1,1024]{1,0:T(1,128)} %bitcast.5, bf16[96,1024]{1,0:T(8,128)(2,1)} %w_qkv_hbm.1, bf16[2,12,128,1024]{3,2,1,0:T(8,128)(2,1)} %cache_hbm.1, bf16[2,12,4,1024]{3,2,1,0:T(4,128)(2,1)} %sink_hbm.1, s32[12]{0:T(128)} %lengths_hbm.1, ...), custom_call_target="tpu_custom_call" | custom-call | tf_op jit(solution)/shard_map/layer/pallas_call | solution.py:697
  55.5 0.7 %reshape.11 = bf16[12,4,1024]{2,1,0:T(4,128)(2,1)} reshape(bf16[48,1024]{1,0:T(8,128)(2,1)S(1)} %layer.1) | data formatting | bytes 196608 | tf_op jit(solution)/shard_map/reshape | solution.py:762

commit v4 on v3

--- a/solution.py
+++ b/solution.py
@@ -64,9 +64,7 @@
     x_tok,
     mix,
     qkv_in,
-    qkv,
     near,
-    q4,
     part_out,
     part_in,
     sinks,
@@ -80,6 +78,8 @@
     back_out,
     back_in,
     fin_in,
+    query_send,
+    query_recv,
     mix_send,
     mix_recv,
     kv_sem,
@@ -118,25 +118,30 @@
     def fetch(at):
         return pltpu.make_async_copy(small[at][0], small[at][1], arg_sem.at[at])
 
+    barrier = pltpu.get_barrier_semaphore()
+
+    def ring4(at, position):
+        return lax.rem(position + ((54 >> (2 * at)) & 3), 4)
+
+    def ring8(at, position):
+        return lax.rem(position + ((0o7162534 >> (3 * at)) & 7), group_count)
+
+    def plane_peer(k):
+        return 8 * ring4(k // 8, col) + 2 * ring4((k // 2) & 3, rg) + lax.rem(core + 1 + k, 2)
+
+    def greet_plane(k, _):
+        pl.semaphore_signal(barrier, inc=1, device_id=(plane_peer(k), z), device_id_type=MESH)
+        return 0
+
+    def greet_line(k, _):
+        pl.semaphore_signal(barrier, inc=1, device_id=(s, ring8(k, z)), device_id_type=MESH)
+        return 0
+
+    lax.fori_loop(0, group_count - 1, greet_line, 0)
+    lax.fori_loop(0, seq_count - 1, greet_plane, 0)
+
     for at in range(len(small)):
         fetch(at).start()
-
-    barrier = pltpu.get_barrier_semaphore()
-
-    def greet_plane(k, _):
-        pl.semaphore_signal(
-            barrier, inc=1, device_id=(lax.rem(s + k, seq_count), z), device_id_type=MESH
-        )
-        return 0
-
-    def greet_line(k, _):
-        pl.semaphore_signal(
-            barrier, inc=1, device_id=(s, lax.rem(z + k, group_count)), device_id_type=MESH
-        )
-        return 0
-
-    lax.fori_loop(1, seq_count, greet_plane, 0)
-    lax.fori_loop(1, group_count, greet_line, 0)
 
     for part in range(3):
         for which in range(2):
@@ -158,15 +163,6 @@
             device_id_type=MESH,
         ).start()
 
-    def ring4(at, position):
-        return lax.rem(position + ((54 >> (2 * at)) & 3), 4)
-
-    def ring8(at, position):
-        return lax.rem(position + ((0o7162534 >> (3 * at)) & 7), group_count)
-
-    def plane_peer(k):
-        return 8 * ring4(k // 8, col) + 2 * ring4((k // 2) & 3, rg) + lax.rem(core + 1 + k, 2)
-
     def to_plane(src, dst, stage):
         def send(k, _):
             rcopy(src, dst, stage, plane_peer(k), z)
@@ -186,12 +182,15 @@
 
     pl.semaphore_wait(barrier, seq_count - 1 + group_count - 1)
 
-    def send_mix(at, dest):
+    qkv_in[s] = mix[...]
+
+    def send_mix(group, send_to, recv_to, dest):
+        rows = pl.ds(pl.multiple_of(16 * group, 16), 16)
         return pltpu.make_async_remote_copy(
-            src_ref=mix,
-            dst_ref=qkv_in.at[s],
-            send_sem=mix_send.at[at],
-            recv_sem=mix_recv.at[s],
+            src_ref=mix.at[rows],
+            dst_ref=qkv_in.at[s, rows],
+            send_sem=send_to,
+            recv_sem=recv_to,
             device_id=(dest, z),
             device_id_type=MESH,
         )
@@ -203,10 +202,12 @@
     @pl.when(has_query)
     def _():
         def send(k, _):
-            send_mix(0, plane_peer(k)).start()
+            group = k // (seq_count - 1)
+            peer = plane_peer(k - group * (seq_count - 1))
+            send_mix(group, query_send.at[0], query_recv.at[group], peer).start()
             return 0
 
-        lax.fori_loop(0, seq_count - 1, send, 0)
+        lax.fori_loop(0, 3 * (seq_count - 1), send, 0)
 
     def each_owner(act):
         for group in range(3):
@@ -215,13 +216,17 @@
                 go = jnp.logical_not(has_query) & (dest != s)
                 if at == 1:
                     go = go & (first_tile != last_tile)
+                place = 2 * (tile // 16) + s - (128 * tile) // 96
 
                 @pl.when(go)
                 def _():
-                    act(send_mix(1 + 2 * group + at, dest))
+                    act(
+                        send_mix(
+                            group, mix_send.at[2 * group + at], mix_recv.at[place], dest
+                        )
+                    )
 
     each_owner(lambda copy: copy.start())
-    qkv_in[s] = mix[...]
     fetch(3).wait()
 
     w_at = 2 * lax.rem(rg, 2) + core
@@ -277,61 +282,55 @@
         for which in range(2):
             sinks[which, 4 * r : 4 * r + 4, :] = sink_ref[which, r].astype(F32)
 
-    lane48 = iota((48, 128), 1)
-
-    def tiles_of(group):
-        last = min(4 * group + 3, QUERY_BLOCKS - 1)
-        b0, b1, b2 = (qkv_in[4 * group + k].astype(F32) for k in range(3))
-        b3 = qkv_in[last].astype(F32)
-        r1 = pltpu.roll(b1, 96, 1)
-        r2 = pltpu.roll(b2, 64, 1)
-        r3 = pltpu.roll(b3, 32, 1)
-        return (
-            jnp.where(lane48 < 96, b0, r1),
-            jnp.where(lane48 < 64, r1, r2),
-            jnp.where(lane48 < 32, r2, r3),
-        )
-
-    def wait_block(block):
-        @pl.when(block != s)
+    def wait_query(group):
+        @pl.when(has_query)
         def _():
-            wait_bytes(qkv_in.at[block], mix_recv.at[block])
-
-    def wait_query(block, _):
-        wait_block(block)
-        return 0
-
-    lax.fori_loop(0, QUERY_BLOCKS, wait_query, 0)
-    tiles = []
-    for group in range(3):
-        for at, tile in enumerate(tiles_of(group)):
-            tiles.append(tile)
-            if 3 * group + at < 8:
-                qkv[3 * group + at] = tile
-    sub6 = iota((6, 8, 128), 1)
-    lane6 = iota((6, 8, 128), 2)
-    diag6 = (sub6 < 4) == (lane6 < 64)
-    zero6 = jnp.zeros((6, 8, 128), F32)
-    for u in range(4):
-        tops = []
-        for tile in (tiles[2 * u], tiles[2 * u + 1]):
-            v = tile.reshape(6, 8, 128)
+            wait_bytes(qkv_in.at[pl.ds(0, QUERY_BLOCKS - 1), pl.ds(0, 16)], query_recv.at[group])
+
+        @pl.when(jnp.logical_not(has_query))
+        def _():
+            wait_bytes(qkv_in.at[pl.ds(0, QUERY_BLOCKS), pl.ds(0, 16)], query_recv.at[group])
+
+    lane16 = iota((16, 128), 1)
+
+    def query_tiles(rows):
+        tiles = []
+        for first in range(0, QUERY_BLOCKS, 4):
+            last = min(first + 3, QUERY_BLOCKS - 1)
+            b0, b1, b2, b3 = (
+                qkv_in[b, rows, :].astype(F32) for b in (first, first + 1, first + 2, last)
+            )
+            r1 = pltpu.roll(b1, 96, 1)
+            r2 = pltpu.roll(b2, 64, 1)
+            r3 = pltpu.roll(b3, 32, 1)
+            tiles.append(jnp.where(lane16 < 96, b0, r1))
+            tiles.append(jnp.where(lane16 < 64, r1, r2))
+            tiles.append(jnp.where(lane16 < 32, r2, r3))
+        return tiles[0:8]
+
+    sub2 = iota((2, 8, 128), 1)
+    lane2 = iota((2, 8, 128), 2)
+    diag2 = (sub2 < 4) == (lane2 < 64)
+    zero = jnp.zeros((8, 128), F32)
+
+    def spread_queries(tiles):
+        parts = []
+        for tile in tiles:
+            v = tile.reshape(2, 8, 128)
             w = pltpu.roll(v, 4, 1)
-            even = jnp.where(diag6, jnp.where(sub6 < 4, v, w), 0.0)
-            odd = jnp.where(diag6, jnp.where(sub6 < 4, w, v), 0.0)
-            tops.append((even, odd))
-        for parity in range(2):
-            upper = jnp.concatenate([tops[0][parity], zero6], axis=2)
-            lower = jnp.concatenate([zero6, tops[1][parity]], axis=2)
-            q4[:, parity, u] = jnp.concatenate([upper, lower], axis=1).astype(BF16)
-
-    for part in range(3):
-        for which in range(2):
-            pltpu.make_async_copy(
-                cache_hbm.at[which, pl.ds(4 * part, 4)],
-                kv.at[which, pl.ds(4 * part, 4)],
-                kv_sem.at[which, part],
-            ).wait()
+            even = jnp.where(diag2, jnp.where(sub2 < 4, v, w), 0.0)
+            odd = jnp.where(diag2, jnp.where(sub2 < 4, w, v), 0.0)
+            parts.append((even, odd))
+        spread = []
+        for pair in range(2):
+            for parity in range(2):
+                row = []
+                for u in range(4):
+                    upper = jnp.concatenate([parts[2 * u][parity][pair], zero], axis=1)
+                    lower = jnp.concatenate([zero, parts[2 * u + 1][parity][pair]], axis=1)
+                    row.append(jnp.concatenate([upper, lower], axis=0).astype(BF16))
+                spread.append(row)
+        return spread
 
     sub8 = iota((8, 8, 128), 1)
     lane8 = iota((8, 8, 128), 2)
@@ -346,68 +345,79 @@
             sub8 < 4, jnp.where(lane8 < 64, a, ar), jnp.where(lane8 < 64, br, b)
         )
 
-    def attend(pair, parity):
-        r = 2 * pair + parity
+    def cache_part(which, group):
+        at = pl.ds(4 * group, 4)
+        return pltpu.make_async_copy(
+            cache_hbm.at[which, at], kv.at[which, at], kv_sem.at[which, group]
+        )
+
+    def attend_rows(group, _):
+        cache_part(0, group).wait()
+        cache_part(1, group).wait()
+        wait_query(group)
+        queries = spread_queries(query_tiles(pl.ds(pl.multiple_of(16 * group, 16), 16)))
         scores = []
-        for u in range(4):
-            scores.append(
-                lax.dot_general(
-                    q4[pair, parity, u],
-                    kv[0, r, :, 256 * u : 256 * u + 256],
-                    LAST,
-                    preferred_element_type=F32,
+        for k in range(4):
+            for u in range(4):
+                scores.append(
+                    lax.dot_general(
+                        queries[k][u],
+                        kv[0, 4 * group + k, :, 256 * u : 256 * u + 256],
+                        LAST,
+                        preferred_element_type=F32,
+                    )
                 )
-            )
-        score = jnp.concatenate(scores, axis=0).reshape(8, 8, 128) * (HD ** (-0.5))
-        held = lengths_ref[r] - SINKS
-        age = (slot_id - held) & (WIN - 1)
-        live = ((slot_id < jnp.minimum(WIN, held)) & (age > step_id))[None]
+        score = jnp.concatenate(scores, axis=0).reshape(4, 8, 8, 128) * (HD ** (-0.5))
+        lives = []
+        for k in range(4):
+            held = lengths_ref[4 * group + k] - SINKS
+            age = (slot_id - held) & (WIN - 1)
+            lives.append(((slot_id < jnp.minimum(WIN, held)) & (age > step_id)).astype(F32))
+        live = jnp.concatenate(lives, axis=0).reshape(4, 1, 8, 128) > 0.0
         peak = jnp.max(jnp.where(live, score, MASKED), axis=-1, keepdims=True)
         weight = jnp.where(live, jnp.exp(score - peak), 0.0)
         total = jnp.sum(weight, axis=-1, keepdims=True)
-        rounded = weight.reshape(64, 128).astype(BF16)
+        rounded = weight.reshape(256, 128).astype(BF16)
         values = []
-        for u in range(4):
-            mixed = jnp.dot(
-                rounded[16 * u : 16 * u + 16],
-                kv[1, r, :, 256 * u : 256 * u + 256],
-                preferred_element_type=F32,
-            )
-            values.append(mixed[0:8, 0:128])
-            values.append(mixed[8:16, 128:256])
-        value = jnp.concatenate(values, axis=0).reshape(8, 8, 128)
-        peak = jnp.broadcast_to(peak, (8, 8, 128))
-        total = jnp.broadcast_to(total, (8, 8, 128))
+        for k in range(4):
+            found = []
+            for u in range(4):
+                at = 64 * k + 16 * u
+                mixed = jnp.dot(
+                    rounded[at : at + 16],
+                    kv[1, 4 * group + k, :, 256 * u : 256 * u + 256],
+                    preferred_element_type=F32,
+                )
+                found.append(mixed[0:8, 0:128])
+                found.append(mixed[8:16, 128:256])
+            values.append(jnp.concatenate(found, axis=0).reshape(8, 8, 128))
+        peak = jnp.broadcast_to(peak, (4, 8, 8, 128))
+        total = jnp.broadcast_to(total, (4, 8, 8, 128))
         p_hi = peak.astype(BF16).astype(F32)
         p_mid = (peak - p_hi).astype(BF16).astype(F32)
         p_low = peak - p_hi - p_mid
         t_hi = total.astype(BF16).astype(F32)
         t_low = total - t_hi
+        lane_at = lane_in[None]
         stat = jnp.where(
-            lane_in == 0,
+            lane_at == 0,
             p_hi,
             jnp.where(
-                lane_in == 1,
+                lane_at == 1,
                 p_mid,
                 jnp.where(
-                    lane_in == 2,
+                    lane_at == 2,
                     p_low,
-                    jnp.where(lane_in == 3, t_hi, jnp.where(lane_in == 4, t_low, 0.0)),
+                    jnp.where(lane_at == 3, t_hi, jnp.where(lane_at == 4, t_low, 0.0)),
                 ),
             ),
         )
-        return value, stat
-
-    def attend_rows(group, _):
-        halves = []
-        for at in range(2):
-            va, sa = attend(2 * group + at, 0)
-            vb, sb = attend(2 * group + at, 1)
-            halves.append((merge(va, vb), merge(sa, sb)))
-        value = jnp.concatenate([halves[0][0], halves[1][0]], axis=1).astype(BF16)
-        stat = jnp.concatenate([halves[0][1], halves[1][1]], axis=1).astype(BF16)
-        part_out[group, :, 0:16, :] = value
-        part_out[group, :, 16:32, :] = stat
+        part_out[group, :, 0:16, :] = jnp.concatenate(
+            [merge(values[0], values[1]), merge(values[2], values[3])], axis=1
+        ).astype(BF16)
+        part_out[group, :, 16:32, :] = jnp.concatenate(
+            [merge(stat[0], stat[1]), merge(stat[2], stat[3])], axis=1
+        ).astype(BF16)
 
         def send(k, _):
             tile = 2 * ring4(k // 2, col) + lax.rem(core + k, 2)
@@ -437,23 +447,23 @@
         part_in[s] = part_out[rg, t]
         rows = pl.ds(pl.multiple_of(16 * rg, 16), 16)
         lanes = pl.ds(pl.multiple_of(128 * t, 128), 128)
-        q_own = qkv[t, rows, :]
 
         def own_tile(tile):
             block = (128 * tile) // 96
             offset = 128 * tile - 96 * block
-            for b in (block, block + 1):
-
-                @pl.when(b >= QUERY_BLOCKS)
+            for k in range(2):
+
+                @pl.when((block + k >= QUERY_BLOCKS) & (block + k != s))
                 def _():
-                    wait_block(b)
+                    wait_bytes(mix.at[pl.ds(0, 16)], mix_recv.at[2 * (tile // 16) + k])
 
             low = pltpu.roll(qkv_in[block, rows, :].astype(F32), 128 - offset, 1)
             high = pltpu.roll(qkv_in[block + 1, rows, :].astype(F32), 96 - offset, 1)
-            return jnp.where(iota((16, 128), 1) < 96 - offset, low, high).astype(BF16)
-
-        k_own = own_tile(8 + t)
-        v_own = own_tile(16 + t)
+            return jnp.where(lane16 < 96 - offset, low, high)
+
+        q_own = own_tile(t)
+        k_own = own_tile(8 + t).astype(BF16)
+        v_own = own_tile(16 + t).astype(BF16)
         k_sink = sinks[0, rows, lanes].astype(BF16)
         v_sink = sinks[1, rows, lanes].astype(BF16)
         rep_row = iota((64, 16), 0)
@@ -641,7 +651,7 @@
 
     @pl.when(has_query)
     def _():
-        wait_bytes(qkv_in.at[pl.ds(0, seq_count - 1)], mix_send.at[0])
+        wait_bytes(qkv_in.at[pl.ds(0, seq_count - 1)], query_send.at[0])
 
     each_owner(lambda copy: copy.wait_send())
 
@@ -716,9 +726,7 @@
                 pltpu.VMEM((48, 1024), F32),
                 pltpu.VMEM((48, 128), BF16),
                 pltpu.VMEM((32, 48, 128), BF16),
-                pltpu.VMEM((8, 48, 128), F32),
                 pltpu.VMEM((3, 16, 128), F32),
-                pltpu.VMEM((6, 2, 4, 16, 256), BF16),
                 pltpu.VMEM((3, 8, 32, 128), BF16),
                 pltpu.VMEM((32, 32, 128), BF16),
                 pltpu.VMEM((2, 48, 1024), F32),
@@ -732,8 +740,10 @@
                 pltpu.VMEM((4, 8, 128), BF16),
                 pltpu.VMEM((8, 8, 128), BF16),
                 pltpu.VMEM((32, 24, 128), BF16),
-                pltpu.SemaphoreType.DMA((7,)),
-                pltpu.SemaphoreType.DMA((32,)),
+                pltpu.SemaphoreType.DMA((1,)),
+                pltpu.SemaphoreType.DMA((3,)),
+                pltpu.SemaphoreType.DMA((6,)),
+                pltpu.SemaphoreType.DMA((4,)),
                 pltpu.SemaphoreType.DMA((2, 3)),
                 pltpu.SemaphoreType.DMA((2,)),
                 pltpu.SemaphoreType.DMA((10,)),

time: 56.3 us -> 52.9 us (0.940)
  Pallas kernels: 55.5 us -> 52.1 us
    pallas_call x1, Pallas kernels: 55.5 us -> 52.1 us  [body(): pl.pallas_call(functools.partial(layer_kernel, seq_count, group_count), o...]
where the time goes in v4:
time: 52.9 us; the launch traced here: 52.8 us
  Pallas kernels  52.1 us (98%)
  local copies, waits for them, and re-layouts  0.68 us (1%)
    pallas_call x1, Pallas kernels, body(): pl.pallas_call(functools.partial(layer_kernel, seq_count, group_count), o...  52.1 us

profile of v4, /device:TPU:1, one launch (start us, length us, event | category | flops | bytes accessed | tf_op | source)
XLA Modules:
  0.0 52.8 jit_solution(11273546062838572415)
XLA Ops:
  0.0 52.1 %layer.1 = bf16[48,1024]{1,0:T(8,128)(2,1)S(1)} custom-call(bf16[12,4,1024]{2,1,0:T(4,128)(2,1)} %tokens_hbm.1, f32[1,1024]{1,0:T(1,128)} %bitcast.5, bf16[96,1024]{1,0:T(8,128)(2,1)} %w_qkv_hbm.1, bf16[2,12,128,1024]{3,2,1,0:T(8,128)(2,1)} %cache_hbm.1, bf16[2,12,4,1024]{3,2,1,0:T(4,128)(2,1)} %sink_hbm.1, s32[12]{0:T(128)} %lengths_hbm.1, ...), custom_call_target="tpu_custom_call" | custom-call | tf_op jit(solution)/shard_map/layer/pallas_call | solution.py:707
  52.1 0.7 %reshape.11 = bf16[12,4,1024]{2,1,0:T(4,128)(2,1)} reshape(bf16[48,1024]{1,0:T(8,128)(2,1)S(1)} %layer.1) | data formatting | bytes 196608 | tf_op jit(solution)/shard_map/reshape | solution.py:772

commit v5 on v4

--- a/solution.py
+++ b/solution.py
@@ -231,12 +231,12 @@
 
     w_at = 2 * lax.rem(rg, 2) + core
 
-    @pl.when(owner & own_rows)
+    @pl.when(own_rows)
     def _():
         w_rows[w_at] = w_out_ref[...]
 
-    for group in range(3):
-        w_dest = 8 * col + 2 * group + rg // 2
+    for row in range(4):
+        w_dest = 8 * col + 2 * row + rg // 2
 
         @pl.when(w_dest != s)
         def _():
@@ -261,13 +261,13 @@
         id_cols.append(jnp.sum(spread_ids, axis=1, keepdims=True))
         onehots.append((expert_lane == id_cols[c]).astype(F32))
     counts = jnp.dot(earlier, (onehots[0] + onehots[1]).astype(BF16), preferred_element_type=F32)
-    sel_rows = iota((64, 48), 0)
-    sel_expert = 2 * (sel_rows // CAP) + half
+    sel_rows = iota((128, 48), 0)
+    sel_expert = 2 * ((sel_rows // CAP) % 8) + sel_rows // 64
     sel_slot = sel_rows % CAP
     col_ids = iota((48, 64), 1)
     col_expert = 2 * (col_ids // CAP) + half
     col_slot = col_ids % CAP
-    dispatch = jnp.zeros((64, 48), F32)
+    dispatch = jnp.zeros((128, 48), F32)
     picks = []
     for c in range(2):
         pos_col = jnp.sum(onehots[c] * counts, axis=1, keepdims=True).astype(jnp.int32)
@@ -434,14 +434,6 @@
 
     lax.fori_loop(0, 3, attend_rows, 0)
 
-    @pl.when(owner & own_rows)
-    def _():
-        wait_bytes(w_rows.at[pl.ds(0, 3)], recv_sem.at[1])
-
-    @pl.when(owner & jnp.logical_not(own_rows))
-    def _():
-        wait_bytes(w_rows, recv_sem.at[1])
-
     @pl.when(owner)
     def _():
         part_in[s] = part_out[rg, t]
@@ -531,54 +523,57 @@
         value = (
             jnp.sum(factor * part_in[:, 0:16, :].astype(F32), axis=0) + near_factor * near_value
         )
-        att_in[t] = (value / total).astype(BF16)
-
-        def send_att(k, _):
-            tile = 2 * ring4(k // 2, col) + lax.rem(core + 1 + k, 2)
-            rcopy(att_in.at[t], att_in.at[t], 3, holder(tile, rg), z)
-            return 0
-
-        lax.fori_loop(0, 7, send_att, 0)
-        wait_bytes(att_in.at[pl.ds(0, 7)], recv_sem.at[3])
-
-
-    @pl.when(owner)
-    def _():
-        attended = jnp.concatenate([att_in[k] for k in range(8)], axis=1)
-        weights = w_rows[...].reshape(128, 1024)
-        proj_in[8 * rg + t] = lax.dot_general(
-            attended, weights, LAST, preferred_element_type=F32
-        ).astype(BF16)
-        to_plane(proj_in.at[8 * rg + t], proj_in.at[8 * rg + t], 4)
-        wait_bytes(proj_in.at[pl.ds(0, 23)], recv_sem.at[4])
-
-    @pl.when(rg == 3)
-    def _():
-        wait_bytes(proj_in, recv_sem.at[4])
-
-
-    projected = jnp.concatenate(
-        [
-            jnp.concatenate([proj_in[8 * g + k] for k in range(8)], axis=1)
-            for g in range(3)
-        ],
-        axis=0,
+        att_in[8 * rg + t] = (value / total).astype(BF16)
+        to_plane(att_in.at[8 * rg + t], att_in.at[8 * rg + t], 3)
+        wait_bytes(att_in.at[pl.ds(0, 23)], recv_sem.at[3])
+
+    @pl.when(jnp.logical_not(owner))
+    def _():
+        wait_bytes(att_in, recv_sem.at[3])
+
+    @pl.when(own_rows)
+    def _():
+        wait_bytes(w_rows.at[pl.ds(0, 3)], recv_sem.at[1])
+
+    @pl.when(jnp.logical_not(own_rows))
+    def _():
+        wait_bytes(w_rows, recv_sem.at[1])
+
+    attended = jnp.concatenate(
+        [jnp.concatenate([att_in[8 * g + k] for k in range(8)], axis=1) for g in range(3)], axis=0
     )
+    proj_in[t] = lax.dot_general(
+        attended, w_rows[...].reshape(128, 1024), LAST, preferred_element_type=F32
+    ).astype(BF16)
+    own_lanes = pl.ds(pl.multiple_of(128 * t, 128), 128)
+    own_tile_rows = (x_tok[:, own_lanes] + proj_in[t].astype(F32)).astype(BF16)
+    buffer = jnp.dot(dispatch, own_tile_rows, preferred_element_type=F32)
+    disp_out[...] = buffer.reshape(16, 8, 128).astype(BF16)
+
+    def send_rows(k, _):
+        dest_z = ring8(k // 8, z)
+        dest_col = ring4((k // 2) & 3, col)
+        dest_s = 8 * dest_col + 2 * rg + lax.rem(core + 1 + k, 2)
+        rcopy(
+            disp_out.at[8 * (dest_col // 2) + dest_z], disp_in.at[8 * t + z], 5, dest_s, dest_z
+        )
+        return 0
+
+    lax.fori_loop(0, 8 * group_count - 1, send_rows, 0)
+    disp_in[8 * t + z] = disp_out[8 * half + z]
+
+    def send_proj(k, _):
+        tile = 2 * ring4(k // 2, col) + lax.rem(core + 1 + k, 2)
+        rcopy(proj_in.at[t], proj_in.at[t], 4, holder(tile, rg), z)
+        return 0
+
+    lax.fori_loop(0, 7, send_proj, 0)
+    wait_bytes(proj_in.at[pl.ds(0, 7)], recv_sem.at[4])
+    projected = jnp.concatenate([proj_in[k] for k in range(8)], axis=1)
     residual = x_tok[...] + projected.astype(F32)
     x_tok[...] = residual
     inverse = lax.rsqrt(jnp.mean(residual * residual, axis=-1, keepdims=True) + EPSILON)
     normed = (residual * inverse * moe_gain_ref[...]).astype(BF16)
-    own_half = jnp.where(core == 0, normed[:, 0:512], normed[:, 512:1024])
-    buffer = jnp.dot(dispatch, own_half, preferred_element_type=F32)
-    disp_out[...] = buffer.reshape(8, 8, 512).astype(BF16)
-
-    def send_rows(k, _):
-        dest = ring8(k, z)
-        rcopy(disp_out.at[dest], disp_in.at[core, z], 5, s, dest)
-        return 0
-
-    lax.fori_loop(0, group_count - 1, send_rows, 0)
-    disp_in[core, z] = disp_out[z]
 
     logits = lax.dot_general(normed, router_ref[...], LAST, preferred_element_type=F32)
     gates = jnp.zeros((48, 64), F32)
@@ -590,12 +585,12 @@
 
     pltpu.make_async_copy(in_hbm.at[:, 0], win, wt_sem.at[0]).wait()
     pltpu.make_async_copy(down_hbm.at[0], down, wt_sem.at[1]).wait()
-    wait_bytes(disp_in.at[0, pl.ds(0, group_count - 1)], recv_sem.at[5])
-    rcopy(disp_in.at[core], disp_in.at[core], 9, s + 1 - 2 * core, z)
-    wait_bytes(disp_in.at[0], recv_sem.at[9])
-    rows_in = jnp.concatenate(
-        [disp_in[c].astype(F32).reshape(64, 512).astype(BF16) for c in range(2)], axis=1
+    wait_bytes(disp_in.at[pl.ds(0, 8 * group_count - 1)], recv_sem.at[5])
+    raw = jnp.concatenate(
+        [disp_in[8 * k : 8 * k + 8].astype(F32).reshape(64, 128) for k in range(8)], axis=1
     )
+    inverse = lax.rsqrt(jnp.mean(raw * raw, axis=-1, keepdims=True) + EPSILON)
+    rows_in = (raw * inverse * moe_gain_ref[...]).astype(BF16)
     gate_part = lax.dot_general(rows_in, win[0], LAST, preferred_element_type=F32)
     up_part = lax.dot_general(rows_in, win[1], LAST, preferred_element_type=F32)
     hidden = (jax.nn.gelu(gate_part, approximate=True) * up_part).astype(BF16)
@@ -655,26 +650,25 @@
 
     each_owner(lambda copy: copy.wait_send())
 
-    @pl.when(owner & own_rows)
-    def _():
-        wait_bytes(w_rows.at[pl.ds(0, 2)], send_sem.at[1])
-
-    @pl.when(jnp.logical_not(owner & own_rows))
+    @pl.when(own_rows)
     def _():
         wait_bytes(w_rows.at[pl.ds(0, 3)], send_sem.at[1])
 
+    @pl.when(jnp.logical_not(own_rows))
+    def _():
+        wait_bytes(w_rows, send_sem.at[1])
+
     @pl.when(owner)
     def _():
         wait_bytes(part_in.at[pl.ds(0, 23)], send_sem.at[2])
-        wait_bytes(att_in.at[pl.ds(0, 7)], send_sem.at[3])
-        wait_bytes(part_in.at[pl.ds(0, 31), pl.ds(0, 16)], send_sem.at[4])
+        wait_bytes(part_in.at[pl.ds(0, 31), pl.ds(0, 16)], send_sem.at[3])
 
     @pl.when(jnp.logical_not(owner))
     def _():
         wait_bytes(part_in.at[pl.ds(0, 24)], send_sem.at[2])
 
-    wait_bytes(disp_in.at[0, pl.ds(0, group_count - 1)], send_sem.at[5])
-    wait_bytes(disp_in.at[0], send_sem.at[9])
+    wait_bytes(proj_in.at[pl.ds(0, 7)], send_sem.at[4])
+    wait_bytes(disp_in.at[pl.ds(0, 8 * group_count - 1)], send_sem.at[5])
     wait_bytes(exp_in.at[pl.ds(0, 15)], send_sem.at[6])
     wait_bytes(back_in.at[pl.ds(0, group_count - 1)], send_sem.at[7])
     wait_bytes(fin_in.at[pl.ds(0, seq_count - 1)], send_sem.at[8])
@@ -730,11 +724,11 @@
                 pltpu.VMEM((3, 8, 32, 128), BF16),
                 pltpu.VMEM((32, 32, 128), BF16),
                 pltpu.VMEM((2, 48, 1024), F32),
-                pltpu.VMEM((8, 16, 128), BF16),
+                pltpu.VMEM((24, 16, 128), BF16),
                 pltpu.VMEM((4, 32, 1024), BF16),
-                pltpu.VMEM((24, 16, 128), BF16),
-                pltpu.VMEM((8, 8, 512), BF16),
-                pltpu.VMEM((2, 8, 8, 512), BF16),
+                pltpu.VMEM((8, 48, 128), BF16),
+                pltpu.VMEM((16, 8, 128), BF16),
+                pltpu.VMEM((64, 8, 128), BF16),
                 pltpu.VMEM((16, 32, 128), BF16),
                 pltpu.VMEM((16, 32, 128), BF16),
                 pltpu.VMEM((4, 8, 128), BF16),

time: 52.9 us -> 51.6 us (0.975)
  Pallas kernels: 52.1 us -> 50.8 us
    pallas_call x1, Pallas kernels: 52.1 us -> 50.8 us  [body(): pl.pallas_call(functools.partial(layer_kernel, seq_count, group_count), o...]
where the time goes in v5:
time: 51.6 us; the launch traced here: 51.5 us
  Pallas kernels  50.8 us (98%)
  local copies, waits for them, and re-layouts  0.68 us (1%)
    pallas_call x1, Pallas kernels, body(): pl.pallas_call(functools.partial(layer_kernel, seq_count, group_count), o...  50.8 us

profile of v5, /device:TPU:1, one launch (start us, length us, event | category | flops | bytes accessed | tf_op | source)
XLA Modules:
  0.0 51.5 jit_solution(837326851268078138)
XLA Ops:
  0.0 50.8 %layer.1 = bf16[48,1024]{1,0:T(8,128)(2,1)S(1)} custom-call(bf16[12,4,1024]{2,1,0:T(4,128)(2,1)} %tokens_hbm.1, f32[1,1024]{1,0:T(1,128)} %bitcast.5, bf16[96,1024]{1,0:T(8,128)(2,1)} %w_qkv_hbm.1, bf16[2,12,128,1024]{3,2,1,0:T(8,128)(2,1)} %cache_hbm.1, bf16[2,12,4,1024]{3,2,1,0:T(4,128)(2,1)} %sink_hbm.1, s32[12]{0:T(128)} %lengths_hbm.1, ...), custom_call_target="tpu_custom_call" | custom-call | tf_op jit(solution)/shard_map/layer/pallas_call | solution.py:701
  50.8 0.7 %reshape.11 = bf16[12,4,1024]{2,1,0:T(4,128)(2,1)} reshape(bf16[48,1024]{1,0:T(8,128)(2,1)S(1)} %layer.1) | data formatting | bytes 196608 | tf_op jit(solution)/shard_map/reshape | solution.py:766

commit v6 on v5

--- a/solution.py
+++ b/solution.py
@@ -127,7 +127,7 @@
         return lax.rem(position + ((0o7162534 >> (3 * at)) & 7), group_count)
 
     def plane_peer(k):
-        return 8 * ring4(k // 8, col) + 2 * ring4((k // 2) & 3, rg) + lax.rem(core + 1 + k, 2)
+        return 8 * ring4((k // 2) & 3, col) + 2 * ring4(k // 8, rg) + lax.rem(core + 1 + k, 2)
 
     def greet_plane(k, _):
         pl.semaphore_signal(barrier, inc=1, device_id=(plane_peer(k), z), device_id_type=MESH)
@@ -551,8 +551,8 @@
     disp_out[...] = buffer.reshape(16, 8, 128).astype(BF16)
 
     def send_rows(k, _):
-        dest_z = ring8(k // 8, z)
-        dest_col = ring4((k // 2) & 3, col)
+        dest_z = ring8((k // 2) & 7, z)
+        dest_col = ring4(k // 16, col)
         dest_s = 8 * dest_col + 2 * rg + lax.rem(core + 1 + k, 2)
         rcopy(
             disp_out.at[8 * (dest_col // 2) + dest_z], disp_in.at[8 * t + z], 5, dest_s, dest_z

time: 51.6 us -> 51.1 us (level)
    pallas_call x1, Pallas kernels: 50.8 us -> 50.3 us  [body(): pl.pallas_call(functools.partial(layer_kernel, seq_count, group_count), o...]
where the time goes in v6:
time: 51.1 us; the launch traced here: 51 us
  Pallas kernels  50.3 us (98%)
  local copies, waits for them, and re-layouts  0.68 us (1%)
    pallas_call x1, Pallas kernels, body(): pl.pallas_call(functools.partial(layer_kernel, seq_count, group_count), o...  50.3 us

profile of v6, /device:TPU:1, one launch (start us, length us, event | category | flops | bytes accessed | tf_op | source)
XLA Modules:
  0.0 51.0 jit_solution(3912433143895955923)
XLA Ops:
  0.0 50.3 %layer.1 = bf16[48,1024]{1,0:T(8,128)(2,1)S(1)} custom-call(bf16[12,4,1024]{2,1,0:T(4,128)(2,1)} %tokens_hbm.1, f32[1,1024]{1,0:T(1,128)} %bitcast.5, bf16[96,1024]{1,0:T(8,128)(2,1)} %w_qkv_hbm.1, bf16[2,12,128,1024]{3,2,1,0:T(8,128)(2,1)} %cache_hbm.1, bf16[2,12,4,1024]{3,2,1,0:T(4,128)(2,1)} %sink_hbm.1, s32[12]{0:T(128)} %lengths_hbm.1, ...), custom_call_target="tpu_custom_call" | custom-call | tf_op jit(solution)/shard_map/layer/pallas_call | solution.py:701
  50.3 0.7 %reshape.11 = bf16[12,4,1024]{2,1,0:T(4,128)(2,1)} reshape(bf16[48,1024]{1,0:T(8,128)(2,1)S(1)} %layer.1) | data formatting | bytes 196608 | tf_op jit(solution)/shard_map/reshape | solution.py:766

commit v7 on v6

--- a/solution.py
+++ b/solution.py
@@ -143,13 +143,12 @@
     for at in range(len(small)):
         fetch(at).start()
 
+    def cache_part(group):
+        at = pl.ds(4 * group, 4)
+        return pltpu.make_async_copy(cache_hbm.at[:, at], kv.at[:, at], kv_sem.at[group])
+
     for part in range(3):
-        for which in range(2):
-            pltpu.make_async_copy(
-                cache_hbm.at[which, pl.ds(4 * part, 4)],
-                kv.at[which, pl.ds(4 * part, 4)],
-                kv_sem.at[which, part],
-            ).start()
+        cache_part(part).start()
     pltpu.make_async_copy(in_hbm.at[:, 0], win, wt_sem.at[0]).start()
     pltpu.make_async_copy(down_hbm.at[0], down, wt_sem.at[1]).start()
 
@@ -345,15 +344,8 @@
             sub8 < 4, jnp.where(lane8 < 64, a, ar), jnp.where(lane8 < 64, br, b)
         )
 
-    def cache_part(which, group):
-        at = pl.ds(4 * group, 4)
-        return pltpu.make_async_copy(
-            cache_hbm.at[which, at], kv.at[which, at], kv_sem.at[which, group]
-        )
-
     def attend_rows(group, _):
-        cache_part(0, group).wait()
-        cache_part(1, group).wait()
+        cache_part(group).wait()
         wait_query(group)
         queries = spread_queries(query_tiles(pl.ds(pl.multiple_of(16 * group, 16), 16)))
         scores = []
@@ -738,11 +730,11 @@
                 pltpu.SemaphoreType.DMA((3,)),
                 pltpu.SemaphoreType.DMA((6,)),
                 pltpu.SemaphoreType.DMA((4,)),
-                pltpu.SemaphoreType.DMA((2, 3)),
+                pltpu.SemaphoreType.DMA((3,)),
                 pltpu.SemaphoreType.DMA((2,)),
                 pltpu.SemaphoreType.DMA((10,)),
-                pltpu.SemaphoreType.DMA((10,)),
-                pltpu.SemaphoreType.DMA((10,)),
+                pltpu.SemaphoreType.DMA((9,)),
+                pltpu.SemaphoreType.DMA((9,)),
             ],
             compiler_params=pltpu.CompilerParams(
                 collective_id=0, has_side_effects=True, vmem_limit_bytes=48 * 1024 * 1024

time: 51.1 us -> 51 us (level)
  no operation moved by 1% of the time
where the time goes in v7:
time: 51 us; the launch traced here: 50.9 us
  Pallas kernels  50.3 us (99%)
  local copies, waits for them, and re-layouts  0.68 us (1%)
    pallas_call x1, Pallas kernels, body(): pl.pallas_call(functools.partial(layer_kernel, seq_count, group_count), o...  50.3 us

profile of v7, /device:TPU:1, one launch (start us, length us, event | category | flops | bytes accessed | tf_op | source)
XLA Modules:
  0.0 50.9 jit_solution(14385009576410066897)
XLA Ops:
  0.0 50.3 %layer.1 = bf16[48,1024]{1,0:T(8,128)(2,1)S(1)} custom-call(bf16[12,4,1024]{2,1,0:T(4,128)(2,1)} %tokens_hbm.1, f32[1,1024]{1,0:T(1,128)} %bitcast.5, bf16[96,1024]{1,0:T(8,128)(2,1)} %w_qkv_hbm.1, bf16[2,12,128,1024]{3,2,1,0:T(8,128)(2,1)} %cache_hbm.1, bf16[2,12,4,1024]{3,2,1,0:T(4,128)(2,1)} %sink_hbm.1, s32[12]{0:T(128)} %lengths_hbm.1, ...), custom_call_target="tpu_custom_call" | custom-call | tf_op jit(solution)/shard_map/layer/pallas_call | solution.py:693
  50.3 0.7 %reshape.11 = bf16[12,4,1024]{2,1,0:T(4,128)(2,1)} reshape(bf16[48,1024]{1,0:T(8,128)(2,1)S(1)} %layer.1) | data formatting | bytes 196608 | tf_op jit(solution)/shard_map/reshape | solution.py:758
